TPU v7x, 256 devices: a whole 4x4x8 slice. The times are simulated.
256 devices in a mesh: strike: 64 (over y, z, core), dip: 4 (over x).
Axes of the slice: x: 4, y: 4, z: 8, core: 2. Of those that a mesh axis runs over, the one named last changes fastest.
Arguments:
- slip_rate: float32 [3, 4096, 1024], P(None, 'strike', 'dip'), may hold values from -6 to 6
- history: bfloat16 [4, 3, 2, 1024, 4096], P(None, None, None, ('strike', 'dip')), may hold values from -6 to 6
- lengths: int32 [1024, 4096], P(('strike', 'dip')), may hold values from 1 to 4, as said below
- prestress: float32 [2, 4096, 1024], P(None, 'strike', 'dip'), may hold values from -8 to 8
- normal_stress: float32 [4096, 1024], P('strike', 'dip'), may hold values from 8 to 16
- direct_effect: float32 [4096, 1024], P('strike', 'dip'), may hold values from 0.01 to 0.04
- state_log: float32 [4096, 1024], P('strike', 'dip'), may hold values from 1 to 5
Outputs:
- next_rates: float32 [3, 4096, 1024], P(None, 'strike', 'dip')
- next_state: float32 [4096, 1024], P('strike', 'dip')
Inputs may be any that keep to these rules, and one draw needn't show every extreme that they name: `lengths`: how many of the newest slip-rate spectra enter each wavenumber's stress transfer.
All inputs are finite; a program needn't handle non-finite values.
Results may differ from a plain program's by a relative error of at most 0.0003.
Values sent between devices are 32-bit elements; how exact they have to be, the bound alone decides.
No kernel may reach another device: no remote copies, remote signals or barrier semaphores. Data moves between devices by JAX's collectives and lax.ppermute only.
A program may use at most 128 MiB of HBM per device.

v0:
```python
import math

import jax
import jax.numpy as jnp
from jax import lax
from jax.sharding import PartitionSpec as P

HIST = 4
NEWTON = 2


time_step = 0.5
coupling = 0.5
decay_rate = 0.05
shear_speed = 0.6
opening_speed = 1.7
radiation = 0.5
healing = 1.0
slip_length = 2.0
highest = lax.Precision.HIGHEST


def area_sine(ratio):
    return jnp.log(ratio + jnp.sqrt(ratio * ratio + 1.0))


def wave_geometry(dip_modes, strike_modes, dip_cells, strike_cells):
    signed_dip = jnp.where(2 * dip_modes < dip_cells, dip_modes, dip_modes - dip_cells)
    signed_strike = jnp.where(
        2 * strike_modes < strike_cells, strike_modes, strike_modes - strike_cells
    )
    wave_dip = signed_dip.astype(jnp.float32) * (2.0 * math.pi / dip_cells)
    wave_strike = signed_strike.astype(jnp.float32) * (2.0 * math.pi / strike_cells)
    modulus = jnp.sqrt(wave_strike * wave_strike + wave_dip * wave_dip)
    anchor = (signed_dip == 0) & (signed_strike == 0)
    safe_modulus = jnp.where(anchor, 1.0, modulus)
    unit_strike = jnp.where(anchor, 1.0, wave_strike / safe_modulus)
    unit_dip = jnp.where(anchor, 0.0, wave_dip / safe_modulus)
    return (modulus, unit_strike, unit_dip)


def delay_mixing(geometry, delay):
    modulus, unit_strike, unit_dip = geometry
    phase_arg = modulus * (time_step * (delay + 1.0))
    envelope = -coupling * time_step * modulus * jnp.exp(-decay_rate * phase_arg)
    mode_two = envelope * jnp.cos(phase_arg)
    mode_three = envelope * jnp.cos(shear_speed * phase_arg)
    mode_one = envelope * jnp.cos(opening_speed * phase_arg)
    mix_along = unit_strike * unit_strike * mode_two + unit_dip * unit_dip * mode_three
    mix_cross = unit_strike * unit_dip * (mode_two - mode_three)
    mix_across = unit_dip * unit_dip * mode_two + unit_strike * unit_strike * mode_three
    return (mix_along, mix_cross, mix_across, mode_one)


def delay_term(spectrum, mixing, active):
    mix_along, mix_cross, mix_across, mode_one = mixing
    force_strike = (mix_along * spectrum[0] + mix_cross * spectrum[1]) * active
    force_dip = (mix_cross * spectrum[0] + mix_across * spectrum[1]) * active
    force_open = mode_one * spectrum[2] * active
    return jnp.stack([force_strike, force_dip, force_open])


def friction_step(force_field, prestress, normal_stress, direct_effect, state_log):
    load_strike = prestress[0] + force_field[0]
    load_dip = prestress[1] + force_field[1]
    traction = jnp.sqrt(load_strike * load_strike + load_dip * load_dip)
    strength = direct_effect * normal_stress
    factor = 2.0 * radiation * jnp.exp(-state_log)
    estimate = jnp.minimum(traction / strength, area_sine(traction / factor))
    for repeat in range(NEWTON):
        residual = traction - strength * estimate - factor * jnp.sinh(estimate)
        estimate = estimate + residual / (strength + factor * jnp.cosh(estimate))
    slip_speed = (traction - strength * estimate) / radiation
    unit_scale = slip_speed / jnp.maximum(traction, 1.0)
    new_rates = jnp.stack(
        [unit_scale * load_strike, unit_scale * load_dip, force_field[2] / radiation]
    )
    new_state = state_log + time_step * (healing * jnp.exp(-state_log) - slip_speed / slip_length)
    return (new_rates, new_state)


def phase_table(first_index, second_index, period):
    turn_count = first_index[:, None] * second_index[None, :] % period
    angle_table = turn_count.astype(jnp.float32) * (2.0 * math.pi / period)
    return (jnp.cos(angle_table), jnp.sin(angle_table))


def contract(pattern, first_operand, second_operand):
    return jnp.einsum(pattern, first_operand, second_operand, precision=highest)


def pair_section(part_real, part_imag, pattern, cos_table, sin_table, sign):
    out_real = contract(pattern, part_real, cos_table) - sign * contract(
        pattern, part_imag, sin_table
    )
    out_imag = contract(pattern, part_imag, cos_table) + sign * contract(
        pattern, part_real, sin_table
    )
    return (out_real, out_imag)


def twist_phase(part_real, part_imag, cos_table, sin_table, sign):
    out_real = cos_table * part_real - sign * sin_table * part_imag
    out_imag = cos_table * part_imag + sign * sin_table * part_real
    return (out_real, out_imag)


def shards(slip_rate, history, lengths, prestress, normal_stress, direct_effect, state_log):
    strike_count = lax.axis_size("strike")
    dip_count = lax.axis_size("dip")
    strike_index = lax.axis_index("strike")
    dip_index = lax.axis_index("dip")
    row_count = slip_rate.shape[1]
    dip_block = slip_rate.shape[2]
    mode_rows = history.shape[3]
    strike_cells = history.shape[4]
    dip_cells = dip_block * dip_count
    unit_modes = dip_count * mode_rows
    norm_dip = 1.0 / math.sqrt(dip_cells)
    norm_strike = 1.0 / math.sqrt(strike_cells)
    local_modes = jnp.arange(mode_rows, dtype=jnp.int32)
    dip_modes = (strike_index * dip_count + dip_index) * mode_rows + local_modes
    strike_modes = jnp.arange(strike_cells, dtype=jnp.int32)
    geometry = wave_geometry(dip_modes[:, None], strike_modes[None, :], dip_cells, strike_cells)
    coarse_all = jnp.arange(unit_modes, dtype=jnp.int32)
    coarse_own = dip_index * mode_rows + local_modes
    outer_index = jnp.arange(strike_count, dtype=jnp.int32)
    inner_index = jnp.arange(row_count, dtype=jnp.int32)
    cos_outer, sin_outer = phase_table(outer_index, outer_index, strike_count)
    cos_bend, sin_bend = phase_table(outer_index, inner_index, strike_cells)
    cos_bend = cos_bend * norm_strike
    sin_bend = sin_bend * norm_strike
    cos_inner, sin_inner = phase_table(inner_index, inner_index, row_count)

    def strike_forward(spectral):
        item_count = spectral.shape[0]
        grid_view = spectral.reshape(item_count, 2, mode_rows, strike_count, row_count)
        section_real, section_imag = pair_section(
            grid_view[:, 0], grid_view[:, 1], "ngpr,kp->ngkr", cos_outer, sin_outer, -1.0
        )
        bent_real, bent_imag = twist_phase(section_real, section_imag, cos_bend, sin_bend, -1.0)
        out_real, out_imag = pair_section(
            bent_real, bent_imag, "ngkr,rm->ngmk", cos_inner, sin_inner, -1.0
        )
        return jnp.stack([out_real, out_imag], axis=1).reshape(
            item_count, 2, mode_rows, strike_cells
        )

    def strike_inverse(spectral):
        grid_view = spectral.reshape(3, 2, mode_rows, row_count, strike_count)
        section_real, section_imag = pair_section(
            grid_view[:, 0], grid_view[:, 1], "ngmk,rm->ngrk", cos_inner, sin_inner, 1.0
        )
        bent_real, bent_imag = twist_phase(section_real, section_imag, cos_bend.T, sin_bend.T, 1.0)
        out_real, out_imag = pair_section(
            bent_real, bent_imag, "ngrk,kp->ngpr", cos_outer, sin_outer, 1.0
        )
        return jnp.stack([out_real, out_imag], axis=1).reshape(3, 2, mode_rows, strike_cells)

    def to_modes(space_field):
        gathered = lax.all_gather(space_field, "dip", axis=2, tiled=True)
        cos_first, sin_first = phase_table(coarse_all, coarse_own, unit_modes)
        cos_twist, sin_twist = phase_table(outer_index, coarse_own, dip_cells)
        grid_view = gathered.reshape(3, row_count, unit_modes, strike_count)
        first_real = contract("cxab,au->cxbu", grid_view, cos_first)
        first_imag = -contract("cxab,au->cxbu", grid_view, sin_first)
        bent_real, bent_imag = twist_phase(
            first_real, first_imag, cos_twist * norm_dip, sin_twist * norm_dip, -1.0
        )
        out_real, out_imag = pair_section(
            bent_real, bent_imag, "cxbi,bs->csix", cos_outer, sin_outer, -1.0
        )
        dip_spec = jnp.stack([out_real, out_imag], axis=1).reshape(3, 2, dip_block, row_count)
        return strike_forward(
            lax.all_to_all(dip_spec, "strike", split_axis=2, concat_axis=3, tiled=True)
        )

    def to_space(mode_field):
        mixed_rows = strike_inverse(mode_field)
        dip_spec = lax.all_to_all(mixed_rows, "strike", split_axis=3, concat_axis=2, tiled=True)
        gathered = lax.all_gather(dip_spec, "dip", axis=2, tiled=True)
        grid_view = gathered.reshape(3, 2, dip_count, strike_count, mode_rows, row_count)
        cos_last, sin_last = phase_table(coarse_own, coarse_all, unit_modes)
        first_real, first_imag = pair_section(
            grid_view[:, 0], grid_view[:, 1], "cdsix,bs->cxbdi", cos_outer, sin_outer, 1.0
        )
        first_real = first_real.reshape(3, row_count, strike_count, unit_modes)
        first_imag = first_imag.reshape(3, row_count, strike_count, unit_modes)
        cos_twist, sin_twist = phase_table(outer_index, coarse_all, dip_cells)
        bent_real, bent_imag = twist_phase(
            first_real, first_imag, cos_twist * norm_dip, sin_twist * norm_dip, 1.0
        )
        space_part = contract("cxbu,au->cxab", bent_real, cos_last) - contract(
            "cxbu,au->cxab", bent_imag, sin_last
        )
        return space_part.reshape(3, row_count, dip_block)

    def transfer(recent):
        recent_count = len(recent)
        summed = jnp.zeros(recent[0].shape, jnp.float32)
        for offset in range(HIST):
            if offset < recent_count:
                source = recent[offset]
            else:
                source = history[offset - recent_count].astype(jnp.float32)
            active = (offset < lengths).astype(jnp.float32)
            summed = summed + delay_term(source, delay_mixing(geometry, float(offset)), active)
        return summed

    first_spec = to_modes(slip_rate)
    force_field = to_space(transfer([first_spec]))
    next_rates, next_state = friction_step(
        force_field, prestress, normal_stress, direct_effect, state_log
    )
    second_spec = to_modes(next_rates)
    force_field = to_space(transfer([second_spec, first_spec]))
    next_rates, next_state = friction_step(
        force_field, prestress, normal_stress, direct_effect, next_state
    )
    return (next_rates, next_state)


def solution(mesh):
    return jax.shard_map(
        shards,
        mesh=mesh,
        in_specs=(
            P(None, "strike", "dip"),
            P(None, None, None, ("strike", "dip"), None),
            P(("strike", "dip"), None),
            P(None, "strike", "dip"),
            P("strike", "dip"),
            P("strike", "dip"),
            P("strike", "dip"),
        ),
        out_specs=(P(None, "strike", "dip"), P("strike", "dip")),
        check_vma=False,
    )
```

profile of v0, /device:TPU:1, one launch (start us, length us, event | category | flops | bytes accessed | tf_op | source)
XLA Modules:
  0.0 520.3 jit_solution(6019969516380714102)
XLA Ops:
  7.3 13.1 %all_gather.12 = f32[3,64,1024]{2,1,0:T(8,128)S(1)} all-gather(f32[3,64,256]{2,1,0:T(8,128)} %param.7), channel_id=1, replica_groups=mesh['strike'=64,'dip'=4] {'dip'}, dimensions={2}, use_global_device_ids=true | all-gather | bytes 983040 | tf_op jit(solution)/shard_map/all_gather | solution.py:161
  31.2 13.9 %all-to-all-start = ((f32[64,1,1536]{2,1,0:T(1,128)}), f32[64,1,1536]{2,1,0:T(1,128)S(1)}, u32[]{:S(2)}, u32[]{:S(2)}) async-start(f32[64,1,1536]{2,1,0:T(1,128)} %reshape.1792), calls=%async_computation | async-start | bytes 786432 | tf_op jit(solution)/shard_map/all_to_all | solution.py:175
  45.9 4.1 multiply_add_fusion.20
  84.6 10.5 %copy.366 = f32[3,1,4,4096]{2,1,0,3:T(1,128)} copy(f32[3,1,4,4096]{3,2,0,1:T(4,128)S(1)} %stack.171) | data formatting | bytes 393216 | tf_op jit(solution)/shard_map/stack | solution.py:158
  96.7 10.3 %copy.367 = f32[3,1,4,4096]{2,1,0,3:T(1,128)} copy(f32[3,1,4,4096]{3,2,0,1:T(4,128)S(1)} %stack.172) | data formatting | bytes 393216 | tf_op jit(solution)/shard_map/stack | solution.py:158
  107.0 16.7 %fusion.506 = f32[4096,3,2,4]{3,2,1,0:T(2,128)} fusion(f32[3,1,4,4096]{2,1,0,3:T(1,128)} %copy.367, f32[3,1,4,4096]{2,1,0,3:T(1,128)} %copy.366), kind=kLoop, calls=%fused_computation.664 | loop fusion | flops 98304 | bytes 786432
  123.7 16.7 %reshape.1794 = f32[64,1,1536]{2,1,0:T(1,128)S(1)} reshape(f32[4096,3,2,4]{3,2,1,0:T(2,128)} %fusion.506) | data formatting | bytes 786432
  140.4 24.7 %all_to_all.66 = f32[64,1,1536]{2,1,0:T(1,128)S(1)} all-to-all(f32[64,1,1536]{2,1,0:T(1,128)S(1)} %reshape.1794), channel_id=1, replica_groups=mesh['strike'=64,'dip'=4] {'strike'}, dimensions={0} | all-to-all | bytes 786432 | tf_op jit(solution)/shard_map/all_to_all | solution.py:180
  166.7 21.1 %reshape.1795 = f32[4096,3,2,4]{3,2,1,0:T(2,128)} reshape(f32[64,1536]{1,0:T(8,128)S(1)} %reduce.1) | data formatting | bytes 786432
  187.8 16.1 %copy.455 = f32[3,2,4,64,64]{4,3,2,1,0:T(8,128)S(1)} copy(f32[3,2,4,64,64]{2,1,0,4,3:T(2,128)} %bitcast.476) | data formatting | bytes 786432 | tf_op jit(solution)/shard_map/all_to_all | solution.py:180
  205.5 38.9 %all-gather.3.cloned.1.call-done = f32[3,2,1024,64]{3,2,1,0:T(8,128)} async-done(((f32[3,2,256,64]{3,2,1,0:T(8,128)}), f32[3,2,1024,64]{3,2,1,0:T(8,128)}) %all-gather.3.cloned.1.call-update) | async-done | bytes 1572880 | tf_op jit(solution)/shard_map/all_gather | solution.py:181
  255.9 4.2 convolution_subtract_fusion.1
  267.3 10.6 %all_gather.14 = f32[3,64,1024]{2,1,0:T(8,128)S(1)} all-gather(f32[3,64,256]{2,1,0:T(8,128)S(1)} %pad_maximum_fusion.6), channel_id=1, replica_groups=mesh['strike'=64,'dip'=4] {'dip'}, dimensions={2}, use_global_device_ids=true | all-gather | bytes 983040 | tf_op jit(solution)/shard_map/all_gather | solution.py:161
  288.9 14.7 %all-to-all-start.2 = ((f32[64,1,1536]{2,1,0:T(1,128)}), f32[64,1,1536]{2,1,0:T(1,128)S(1)}, u32[]{:S(2)}, u32[]{:S(2)}) async-start(f32[64,1,1536]{2,1,0:T(1,128)} %reshape.1796), calls=%async_computation.2 | async-start | bytes 786432 | tf_op jit(solution)/shard_map/all_to_all | solution.py:175
  307.8 10.3 %all-to-all-done.2 = f32[64,1,1536]{2,1,0:T(1,128)S(1)} async-done(((f32[64,1,1536]{2,1,0:T(1,128)}), f32[64,1,1536]{2,1,0:T(1,128)S(1)}, u32[]{:S(2)}, u32[]{:S(2)}) %all-to-all-start.2) | async-done | bytes 393248 | tf_op jit(solution)/shard_map/all_to_all | solution.py:175
  336.6 10.3 %copy.396 = f32[3,1,4,4096]{2,1,0,3:T(1,128)} copy(f32[3,1,4,4096]{3,2,0,1:T(4,128)S(1)} %stack.193) | data formatting | bytes 393216 | tf_op jit(solution)/shard_map/stack | solution.py:158
  348.6 10.3 %copy.397 = f32[3,1,4,4096]{2,1,0,3:T(1,128)} copy(f32[3,1,4,4096]{3,2,0,1:T(4,128)S(1)} %stack.194) | data formatting | bytes 393216 | tf_op jit(solution)/shard_map/stack | solution.py:158
  358.8 16.7 %fusion.505 = f32[4096,3,2,4]{3,2,1,0:T(2,128)} fusion(f32[3,1,4,4096]{2,1,0,3:T(1,128)} %copy.397, f32[3,1,4,4096]{2,1,0,3:T(1,128)} %copy.396), kind=kLoop, calls=%fused_computation.663 | loop fusion | flops 98304 | bytes 786432
  375.5 16.7 %reshape.1798 = f32[64,1,1536]{2,1,0:T(1,128)S(1)} reshape(f32[4096,3,2,4]{3,2,1,0:T(2,128)} %fusion.505) | data formatting | bytes 786432
  392.3 20.6 %all_to_all.67 = f32[64,1,1536]{2,1,0:T(1,128)S(1)} all-to-all(f32[64,1,1536]{2,1,0:T(1,128)S(1)} %reshape.1798), channel_id=1, replica_groups=mesh['strike'=64,'dip'=4] {'strike'}, dimensions={0} | all-to-all | bytes 786432 | tf_op jit(solution)/shard_map/all_to_all | solution.py:180
  414.4 21.1 %reshape.1799 = f32[4096,3,2,4]{3,2,1,0:T(2,128)} reshape(f32[64,1536]{1,0:T(8,128)S(1)} %reduce.3) | data formatting | bytes 786432
  435.5 15.9 %copy.467 = f32[3,2,4,64,64]{4,3,2,1,0:T(8,128)S(1)} copy(f32[3,2,4,64,64]{2,1,0,4,3:T(2,128)} %bitcast.477) | data formatting | bytes 786432 | tf_op jit(solution)/shard_map/all_to_all | solution.py:180
  452.9 37.3 %all-gather.5.cloned.1.call-done = f32[3,2,1024,64]{3,2,1,0:T(8,128)} async-done(((f32[3,2,256,64]{3,2,1,0:T(8,128)}), f32[3,2,1024,64]{3,2,1,0:T(8,128)}) %all-gather.5.cloned.1.call-update) | async-done | bytes 1572880 | tf_op jit(solution)/shard_map/all_gather | solution.py:181
  501.7 4.2 convolution_subtract_fusion
  (215 shorter events, 125.9 us)
Async XLA Ops:
  28.9 16.8 %copy-start.34 = (s32[4,4096]{1,0:T(4,128)S(1)}, s32[4,4096]{1,0:T(4,128)}, u32[]{:S(2)}) copy-start(s32[4,4096]{1,0:T(4,128)} %param.9) | copy-start | bytes 196612
  28.9 16.8 %copy-start.33 = (bf16[4,3,2,4,4096]{4,3,2,1,0:T(4,128)(2,1)S(1)}, bf16[4,3,2,4,4096]{4,3,2,1,0:T(4,128)(2,1)}, u32[]{:S(2)}) copy-start(bf16[4,3,2,4,4096]{4,3,2,1,0:T(4,128)(2,1)} %param.8) | copy-start | bytes 2359300
  31.2 32.3 %all-to-all-start = ((f32[64,1,1536]{2,1,0:T(1,128)}), f32[64,1,1536]{2,1,0:T(1,128)S(1)}, u32[]{:S(2)}, u32[]{:S(2)}) async-start(f32[64,1,1536]{2,1,0:T(1,128)} %reshape.1792), calls=%async_computation | async-start | bytes 786432 | tf_op jit(solution)/shard_map/all_to_all | solution.py:175
  45.1 199.3 %all-gather.3.cloned.1.call-start = ((), (), s32[]{:S(2)}) async-start(), calls=%async_computation.4 | async-start | bytes 3932160 | tf_op jit(solution)/shard_map/all_gather | solution.py:181
  63.5 11.3 %copy-start.7 = (f32[4,64,64]{2,1,0:T(8,128)}, f32[4,64,64]{2,1,0:T(8,128)S(1)}, u32[]{:S(2)}) copy-start(f32[4,64,64]{2,1,0:T(8,128)S(1)} %get-tuple-element.73) | copy-start | bytes 196612
  63.5 12.3 %copy-start.1 = (f32[4,64,64]{2,1,0:T(8,128)}, f32[4,64,64]{2,1,0:T(8,128)S(1)}, u32[]{:S(2)}) copy-start(f32[4,64,64]{2,1,0:T(8,128)S(1)} %get-tuple-element.55) | copy-start | bytes 196612
  63.5 12.3 %copy-start.3 = (f32[4,64,64]{2,1,0:T(8,128)}, f32[4,64,64]{2,1,0:T(8,128)S(1)}, u32[]{:S(2)}) copy-start(f32[4,64,64]{2,1,0:T(8,128)S(1)} %get-tuple-element.56) | copy-start | bytes 196612
  63.5 12.3 %copy-start.5 = (f32[4,64,64]{2,1,0:T(8,128)}, f32[4,64,64]{2,1,0:T(8,128)S(1)}, u32[]{:S(2)}) copy-start(f32[4,64,64]{2,1,0:T(8,128)S(1)} %get-tuple-element.58) | copy-start | bytes 196612
  74.8 1.9 copy-start.18
  286.6 17.2 %copy-start.29 = (f32[1,2,4,4096]{3,2,1,0:T(4,128)S(1)}, f32[1,2,4,4096]{3,2,1,0:T(4,128)}, u32[]{:S(2)}) copy-start(f32[1,2,4,4096]{3,2,1,0:T(4,128)} %get-tuple-element.48) | copy-start | bytes 393220
  287.3 16.8 %copy-start.28 = (f32[1,2,4,4096]{3,2,1,0:T(4,128)S(1)}, f32[1,2,4,4096]{3,2,1,0:T(4,128)}, u32[]{:S(2)}) copy-start(f32[1,2,4,4096]{3,2,1,0:T(4,128)} %get-tuple-element.47) | copy-start | bytes 393220
  287.3 16.9 %copy-start.27 = (f32[1,2,4,4096]{3,2,1,0:T(4,128)S(1)}, f32[1,2,4,4096]{3,2,1,0:T(4,128)}, u32[]{:S(2)}) copy-start(f32[1,2,4,4096]{3,2,1,0:T(4,128)} %get-tuple-element.46) | copy-start | bytes 393220
  287.3 17.9 %copy-start.32 = (f32[1,2,4,4096]{3,2,1,0:T(4,128)S(1)}, f32[1,2,4,4096]{3,2,1,0:T(4,128)}, u32[]{:S(2)}) copy-start(f32[1,2,4,4096]{3,2,1,0:T(4,128)} %get-tuple-element.51) | copy-start | bytes 393220
  287.3 18.7 %copy-start.31 = (f32[1,2,4,4096]{3,2,1,0:T(4,128)S(1)}, f32[1,2,4,4096]{3,2,1,0:T(4,128)}, u32[]{:S(2)}) copy-start(f32[1,2,4,4096]{3,2,1,0:T(4,128)} %get-tuple-element.50) | copy-start | bytes 393220
  288.9 18.0 %copy-start.30 = (f32[1,2,4,4096]{3,2,1,0:T(4,128)S(1)}, f32[1,2,4,4096]{3,2,1,0:T(4,128)}, u32[]{:S(2)}) copy-start(f32[1,2,4,4096]{3,2,1,0:T(4,128)} %get-tuple-element.49) | copy-start | bytes 393220
  288.9 29.2 %all-to-all-start.2 = ((f32[64,1,1536]{2,1,0:T(1,128)}), f32[64,1,1536]{2,1,0:T(1,128)S(1)}, u32[]{:S(2)}, u32[]{:S(2)}) async-start(f32[64,1,1536]{2,1,0:T(1,128)} %reshape.1796), calls=%async_computation.2 | async-start | bytes 786432 | tf_op jit(solution)/shard_map/all_to_all | solution.py:175
  303.6 186.7 %all-gather.5.cloned.1.call-start = ((), (), s32[]{:S(2)}) async-start(), calls=%async_computation.5 | async-start | bytes 3932160 | tf_op jit(solution)/shard_map/all_gather | solution.py:181
  325.7 2.9 copy-start.2
  325.7 2.9 copy-start.4
  325.7 2.9 copy-start.6
  325.7 2.9 copy-start.8
  327.2 1.7 copy-start.19
  327.2 1.7 copy-start.20
  327.2 1.7 copy-start.21
  (15 other events, 20.5 us)
Sparse Core Ops, SparseCore 0:
  205.5 38.8 all-gather.2
  453.0 37.1 all-gather.4
where the time goes:
time: 528 us; the launch traced here: 520 us
  local copies, waits for them, and re-layouts  189 us (36%)
  waiting for transfers between devices  86.6 us (16%)
  matrix products  75.4 us (14%)
  blocking collectives  69 us (13%)
  other arithmetic  56.3 us (11%)
  starting transfers between devices  29.3 us (6%)
  between operations  15.2 us (3%)
    unnamed x78, local copies, waits for them, and re-layouts  81.5 us
    all_gather x2, waiting for transfers between devices, to_space(): gathered = lax.all_gather(dip_spec, 'dip', axis=2, tiled=True)  76.3 us
    dot_general x56, matrix products, contract(): return jnp.einsum(pattern, first_operand, second_operand, precision=highest)  75.4 us
    all_to_all x2, blocking collectives, to_space(): lax.all_to_all(mixed_rows, 'strike', split_axis=3, concat_axis=2, tiled=T...  45.3 us
    another operation x8, local copies, waits for them, and re-layouts, strike_inverse(): jnp.stack([out_real, out_imag], axis=1)  42.1 us
    all_to_all x4, local copies, waits for them, and re-layouts, to_space(): lax.all_to_all(mixed_rows, 'strike', split_axis=3, concat_axis=2, tiled=T...  34.9 us
    unnamed x2, other arithmetic  33.4 us
    all_to_all x2, starting transfers between devices, to_modes(): lax.all_to_all(dip_spec, 'strike', split_axis=2, concat_axis=3, tiled=True)  28.6 us
  transfers between devices with their start and end apart: 4, of which 3 were waited for; matrix products, arithmetic and copies ran while one was open for 4% of the time, Pallas kernels for 0%

commit v1 on v0

v1 whole, which is shorter than its diff:
```python
import math

import jax
import jax.numpy as jnp
import numpy as np
from jax import lax
from jax.experimental import pallas as pl
from jax.experimental.pallas import tpu as pltpu
from jax.sharding import PartitionSpec as P

NX, NZ = 4096, 1024
DEV = 256
ROWS = NX // DEV
MODES = NZ // DEV
NEWTON = 2
BOTH = ("strike", "dip")
F32, BF16 = jnp.float32, jnp.bfloat16


def split(value):
    high = value.astype(BF16)
    low = (value - high.astype(F32)).astype(BF16)
    return high, low


def split_table(table):
    table = np.asarray(table, np.float64)
    high = table.astype(np.float32).astype(jnp.bfloat16)
    low = (table - high.astype(np.float64)).astype(np.float32).astype(jnp.bfloat16)
    return np.stack([high, low])


def dft_table():
    index = np.arange(DEV)
    angle = 2 * np.pi * (np.outer(index, index) % DEV) / DEV
    return split_table(np.concatenate([np.cos(angle), np.sin(angle)], 0))


def inner_table(sign):
    angle = 2 * np.pi * (np.outer(np.arange(ROWS), np.arange(ROWS)) % ROWS) / ROWS
    cos, sin = np.cos(angle) / math.sqrt(NX), sign * np.sin(angle) / math.sqrt(NX)
    table = np.zeros((2, ROWS, MODES, 2, MODES, ROWS))
    for m in range(MODES):
        table[0, :, m, 0, m, :] = cos
        table[0, :, m, 1, m, :] = -sin
        table[1, :, m, 0, m, :] = sin
        table[1, :, m, 1, m, :] = cos
    return table.reshape(128, 128)


def twist_table():
    angle = 2 * np.pi * np.outer(np.arange(ROWS), np.arange(DEV)) / NX
    return np.stack([np.cos(angle), np.sin(angle)]).astype(np.float32)


def turn_table():
    angle = 2 * np.pi * np.outer(np.arange(MODES), np.arange(DEV)) / NZ
    table = np.stack([np.cos(angle), np.sin(angle)]) / math.sqrt(NZ)
    return table.reshape(2 * MODES, DEV).astype(np.float32)


def dot3(left, right):
    lh, ll = left
    rh, rl = right
    out = jnp.dot(lh, rh, preferred_element_type=F32)
    out += jnp.dot(ll, rh, preferred_element_type=F32)
    out += jnp.dot(lh, rl, preferred_element_type=F32)
    return out


def long_dft(blocks, dft, sign):
    rows = []
    for real, imag in blocks:
        if sign < 0:
            rows.append(jnp.concatenate([real, imag], 1))
            rows.append(jnp.concatenate([imag, -real], 1))
        else:
            rows.append(jnp.concatenate([real, -imag], 1))
            rows.append(jnp.concatenate([imag, real], 1))
    out = dot3(split(jnp.concatenate(rows, 0)), (dft[0], dft[1]))
    return [(out[128 * c : 128 * c + 64], out[128 * c + 64 : 128 * c + 128]) for c in range(3)]


def read_lines(ref):
    blocks = []
    for c in range(3):
        lines = ref[pl.ds(c, DEV, stride=3), :].T
        blocks.append((lines[:64], lines[64:]))
    return blocks


def write_lines(ref, blocks):
    for c, (real, imag) in enumerate(blocks):
        ref[pl.ds(c, DEV, stride=3), :] = jnp.concatenate([real, imag], 0).T


def dip_forward(field, turn):
    cos = [turn[m : m + 1, :] for m in range(4)]
    sin = [turn[4 + m : 5 + m, :] for m in range(4)]
    blocks = []
    for x0, x1, x2, x3 in field:
        even, odd, f, g = x0 + x2, x1 + x3, x0 - x2, x1 - x3
        y0, y2 = even + odd, even - odd
        real = [y0 * cos[0], f * cos[1] - g * sin[1], y2 * cos[2], f * cos[3] + g * sin[3]]
        imag = [
            jnp.zeros_like(y0),
            -(f * sin[1] + g * cos[1]),
            -(y2 * sin[2]),
            g * cos[3] - f * sin[3],
        ]
        blocks.append((jnp.concatenate(real, 0), jnp.concatenate(imag, 0)))
    return blocks


def dip_inverse(blocks, turn):
    cos = [turn[m : m + 1, :] for m in range(4)]
    sin = [turn[4 + m : 5 + m, :] for m in range(4)]
    field = []
    for real, imag in blocks:
        re = [real[16 * m : 16 * m + 16] for m in range(4)]
        im = [imag[16 * m : 16 * m + 16] for m in range(4)]
        u = [cos[m] * re[m] - sin[m] * im[m] for m in range(4)]
        v1 = cos[1] * im[1] + sin[1] * re[1]
        v3 = cos[3] * im[3] + sin[3] * re[3]
        a, b, c, d = u[0] + u[2], u[0] - u[2], u[1] + u[3], v3 - v1
        field.append([a + c, b + d, a - c, b - d])
    return field


def friction(force, prestress, strength, state):
    load_strike = prestress[0] + force[0]
    load_dip = prestress[1] + force[1]
    traction = jnp.sqrt(load_strike * load_strike + load_dip * load_dip)
    factor = jnp.exp(-state)
    ratio = traction / factor
    estimate = jnp.minimum(traction / strength, jnp.log(ratio + jnp.sqrt(ratio * ratio + 1.0)))
    for _ in range(NEWTON):
        up, down = jnp.exp(estimate), jnp.exp(-estimate)
        half = 0.5 * factor
        residual = traction - strength * estimate - half * (up - down)
        estimate = estimate + residual / (strength + half * (up + down))
    slip_speed = 2.0 * (traction - strength * estimate)
    scale = slip_speed / jnp.maximum(traction, 1.0)
    rates = [scale * load_strike, scale * load_dip, 2.0 * force[2]]
    return rates, state + 0.5 * (factor - 0.5 * slip_speed)


def pack_kernel(slip, prestress, normal, effect, state, out):
    for d in range(4):
        rows = slice(16 * d, 16 * d + 16)
        for c in range(3):
            out[d, 16 * c : 16 * c + 16, :] = slip[c, rows, :]
        for c in range(2):
            out[d, 48 + 16 * c : 64 + 16 * c, :] = prestress[c, rows, :]
        out[d, 80:96, :] = normal[rows, :] * effect[rows, :]
        out[d, 96:112, :] = state[rows, :]


def first_kernel(fields, turn, dft, out):
    field = [[fields[d, 16 * c : 16 * c + 16, :] for d in range(4)] for c in range(3)]
    write_lines(out, long_dft(dip_forward(field, turn), dft, -1))


def space_step(lines, fields, state, turn, dft):
    field = dip_inverse(long_dft(read_lines(lines), dft, 1), turn)
    force = [jnp.concatenate(f, 0) for f in field]

    def quarter(at):
        return jnp.concatenate([fields[d, at : at + 16, :] for d in range(4)], 0)

    return friction(force, (quarter(48), quarter(64)), quarter(80), state(quarter))


def middle_kernel(lines, fields, turn, dft, out, state_out):
    rates, state = space_step(lines, fields, lambda quarter: quarter(96), turn, dft)
    state_out[...] = state
    field = [[r[16 * d : 16 * d + 16] for d in range(4)] for r in rates]
    write_lines(out, long_dft(dip_forward(field, turn), dft, -1))


def last_kernel(lines, fields, state_in, turn, dft, out):
    rates, state = space_step(lines, fields, lambda quarter: state_in[...], turn, dft)
    for d in range(4):
        for c, value in enumerate(rates + [state]):
            out[d, 16 * c : 16 * c + 16, :] = value[16 * d : 16 * d + 16]


def unpack_kernel(gathered, rates, state):
    for d in range(4):
        rows = slice(16 * d, 16 * d + 16)
        for c in range(3):
            rates[c, rows, :] = gathered[d, 16 * c : 16 * c + 16, :]
        state[rows, :] = gathered[d, 48:64, :]


def mixing(device):
    shape = (64, DEV)
    row = lax.broadcasted_iota(jnp.int32, shape, 0)
    kx = (row >> 2) * DEV + lax.broadcasted_iota(jnp.int32, shape, 1)
    kz = device * MODES + (row & 3)
    mz = jnp.where(2 * kz < NZ, kz, kz - NZ)
    mx = jnp.where(2 * kx < NX, kx, kx - NX)
    qz = mz.astype(F32) * (2.0 * math.pi / NZ)
    qx = mx.astype(F32) * (2.0 * math.pi / NX)
    q = jnp.sqrt(qx * qx + qz * qz)
    anchor = (mz == 0) & (mx == 0)
    safe = jnp.where(anchor, 1.0, q)
    ex = jnp.where(anchor, 1.0, qx / safe)
    ez = jnp.where(anchor, 0.0, qz / safe)
    xx, xz, zz = ex * ex, ex * ez, ez * ez
    decay = jnp.exp(-0.025 * q)
    envelope = -0.25 * q
    first = [jnp.cos(0.5 * s * q) for s in (1.0, 0.6, 1.7)]
    before = [jnp.ones(shape, F32)] * 3
    now = first
    out = []
    for lag in range(4):
        envelope = envelope * decay
        two, three, one = [envelope * c for c in now]
        out.append((xx * two + zz * three, xz * (two - three), zz * two + xx * three, one))
        now, before = [2.0 * f * c - p for f, c, p in zip(first, now, before)], now
    return out


def history_kernel(history, lengths, past1, past2, coef, held, reach):
    device = lax.axis_index("strike") * 4 + lax.axis_index("dip")
    for k1 in range(16):
        lanes = slice(DEV * k1, DEV * k1 + DEV)
        rows = slice(4 * k1, 4 * k1 + 4)
        reach[rows, :] = lengths[:, lanes].astype(F32)
    for lag in range(3):
        for c in range(3):
            for part in range(2):
                line = history[lag, c, part].astype(F32)
                for k1 in range(16):
                    held[lag, c, part, 4 * k1 : 4 * k1 + 4, :] = line[:, DEV * k1 : DEV * k1 + DEV]
    mix = mixing(device)
    length = reach[...]
    masked = [None] + [
        [jnp.where(length > float(lag), m, 0.0) for m in mix[lag]] for lag in range(1, 4)
    ]
    for i in range(4):
        coef[i] = mix[0][i]
        coef[4 + i] = masked[1][i]
    for out, skip in ((past1, 1), (past2, 2)):
        for part in range(2):
            total = [0.0, 0.0, 0.0]
            for lag in range(skip, 4):
                ss, sd, dd, op = masked[lag]
                a, b, c = [held[lag - skip, i, part] for i in range(3)]
                total[0] = total[0] + (ss * a + sd * b)
                total[1] = total[1] + (sd * a + dd * b)
                total[2] = total[2] + op * c
            for i in range(3):
                out[i, 64 * part : 64 * part + 64, :] = total[i]


def spectrum_of(lines, twist, dft, inner):
    blocks = long_dft(read_lines(lines), dft, -1)
    cos = jnp.concatenate([twist[0]] * 4, 0)
    sin = jnp.concatenate([twist[1]] * 4, 0)
    turned = [
        jnp.concatenate([re * cos + im * sin, im * cos - re * sin], 0) for re, im in blocks
    ]
    return dot3((inner[0], inner[1]), split(jnp.concatenate(turned, 1)))


def lines_of(out, force, twist, dft, inner):
    blocks = dot3((inner[0], inner[1]), split(jnp.concatenate(force, 1)))
    cos = jnp.concatenate([twist[0]] * 4, 0)
    sin = jnp.concatenate([twist[1]] * 4, 0)
    turned = []
    for c in range(3):
        re, im = blocks[:64, DEV * c : DEV * c + DEV], blocks[64:, DEV * c : DEV * c + DEV]
        turned.append((re * cos - im * sin, im * cos + re * sin))
    write_lines(out, long_dft(turned, dft, 1))


def apply_mix(coef, at, spec):
    both = [jnp.concatenate([coef[at + i]] * 2, 0) for i in range(4)]
    s, d, o = [spec[:, DEV * c : DEV * c + DEV] for c in range(3)]
    return [both[0] * s + both[1] * d, both[1] * s + both[2] * d, both[3] * o]


def mode_kernel_first(lines, past, coef, twist, dft, inner, back, out, spec_out):
    spec = spectrum_of(lines, twist, dft, inner)
    spec_out[...] = spec
    force = [f + past[c] for c, f in enumerate(apply_mix(coef, 0, spec))]
    lines_of(out, force, twist, dft, back)


def mode_kernel_second(lines, past, coef, older, twist, dft, inner, back, out):
    spec = spectrum_of(lines, twist, dft, inner)
    new, old = apply_mix(coef, 0, spec), apply_mix(coef, 4, older)
    force = [new[c] + old[c] + past[c] for c in range(3)]
    lines_of(out, force, twist, dft, back)


def call(kernel, outs, *args, scratch=()):
    return pl.pallas_call(
        kernel,
        out_shape=[jax.ShapeDtypeStruct(s, F32) for s in outs],
        scratch_shapes=scratch,
    )(*args)


def exchange(lines):
    return lax.all_to_all(lines.reshape(DEV, 1, 384), BOTH, 0, 0, tiled=True).reshape(768, 128)


def shards(slip_rate, history, lengths, prestress, normal_stress, direct_effect, state_log):
    dft = dft_table()
    inner = split_table(inner_table(-1.0))
    back = split_table(inverse_inner())
    twist, turn = twist_table(), turn_table()
    lines = (768, 128)

    (packed,) = call(
        pack_kernel, [(4, 112, 256)], slip_rate, prestress, normal_stress, direct_effect, state_log
    )
    fields = lax.all_to_all(packed, "dip", 0, 0, tiled=True)
    past1, past2, coef = call(
        history_kernel,
        [(3, 128, 256), (3, 128, 256), (8, 64, 256)],
        history,
        lengths,
        scratch=[pltpu.VMEM((3, 3, 2, 64, 256), F32), pltpu.VMEM((64, 256), F32)],
    )
    (out,) = call(first_kernel, [lines], fields, turn, dft)
    out, spec = call(
        mode_kernel_first, [lines, (128, 768)], exchange(out), past1, coef, twist, dft, inner, back
    )
    out, state = call(
        middle_kernel, [lines, (64, 256)], exchange(out), fields, turn, dft
    )
    (out,) = call(
        mode_kernel_second, [lines], exchange(out), past2, coef, spec, twist, dft, inner, back
    )
    (out,) = call(last_kernel, [(4, 64, 256)], exchange(out), fields, state, turn, dft)
    gathered = lax.all_to_all(out, "dip", 0, 0, tiled=True)
    rates, state = call(unpack_kernel, [(3, 64, 256), (64, 256)], gathered)
    return rates, state


def inverse_inner():
    forward = inner_table(-1.0).reshape(2, ROWS, MODES, 2, MODES, ROWS)
    return forward.transpose(3, 4, 5, 0, 1, 2).reshape(128, 128)


def solution(mesh):
    return jax.shard_map(
        shards,
        mesh=mesh,
        in_specs=(
            P(None, "strike", "dip"),
            P(None, None, None, ("strike", "dip"), None),
            P(("strike", "dip"), None),
            P(None, "strike", "dip"),
            P("strike", "dip"),
            P("strike", "dip"),
            P("strike", "dip"),
        ),
        out_specs=(P(None, "strike", "dip"), P("strike", "dip")),
        check_vma=False,
    )
```

time: 528 us -> 155 us (0.29); the launches traced: 520 us -> 155 us
  local copies, waits for them, and re-layouts: 189 us -> 0.75 us
  matrix products: 75.4 us -> 0 us
  waiting for transfers between devices: 86.6 us -> 15.1 us
  other arithmetic: 56.3 us -> 0 us
  blocking collectives: 69 us -> 98.2 us
  Pallas kernels: 0 us -> 24.6 us
  between operations: 15.2 us -> 0.65 us
  starting transfers between devices: 29.3 us -> 15.5 us
    unnamed x78 -> x2, local copies, waits for them, and re-layouts: 81.5 us -> 0.75 us
    all_gather x2 -> x0, waiting for transfers between devices: 76.3 us -> none  [to_space(): gathered = lax.all_gather(dip_spec, 'dip', axis=2, tiled=True)]
    dot_general x56 -> x0, matrix products: 75.4 us -> none  [contract(): return jnp.einsum(pattern, first_operand, second_operand, precision=highest)]
    another operation x25 -> x0, local copies, waits for them, and re-layouts: 55.5 us -> none  [the longest x8 42.1 us: strike_inverse(): jnp.stack([out_real, out_imag], axis=1)]
    all_to_all x2 -> x5, blocking collectives: 45.3 us -> 98.2 us  [the longest x3 76.8 us: exchange(): lax.all_to_all(lines.reshape(DEV, 1, 384), BOTH, 0, 0, tiled=True)]
    all_to_all x7 -> x0, local copies, waits for them, and re-layouts: 35.8 us -> none  [the longest x4 34.9 us: to_space(): lax.all_to_all(mixed_rows, 'strike', split_axis=3, concat_axis=2, tiled=T...]
    unnamed x2 -> x0, other arithmetic: 33.4 us -> none
    pallas_call x0 -> x8, Pallas kernels: none -> 24.6 us  [call(): pl.pallas_call(kernel, out_shape=[jax.ShapeDtypeStruct(s, F32) for s in o...]
  transfers between devices with their start and end apart: 4 -> 1, of which waited for: 3 -> 1; matrix products, arithmetic and copies ran while one was open for 4% -> 0% of each run, Pallas kernels for 0% -> 2%
where the time goes in v1:
time: 155 us
  blocking collectives  98.2 us (63%)
  Pallas kernels  24.6 us (16%)
  starting transfers between devices  15.5 us (10%)
  waiting for transfers between devices  15.1 us (10%)
    all_to_all x3, blocking collectives, exchange(): lax.all_to_all(lines.reshape(DEV, 1, 384), BOTH, 0, 0, tiled=True)  76.8 us
    pallas_call x8, Pallas kernels, call(): pl.pallas_call(kernel, out_shape=[jax.ShapeDtypeStruct(s, F32) for s in o...  24.6 us
    all_to_all x1, starting transfers between devices, exchange(): lax.all_to_all(lines.reshape(DEV, 1, 384), BOTH, 0, 0, tiled=True)  15.5 us
    all_to_all x1, waiting for transfers between devices, exchange(): lax.all_to_all(lines.reshape(DEV, 1, 384), BOTH, 0, 0, tiled=True)  15.1 us
    all_to_all x1, blocking collectives, shards(): fields = lax.all_to_all(packed, 'dip', 0, 0, tiled=True)  11.5 us
    all_to_all x1, blocking collectives, shards(): gathered = lax.all_to_all(out, 'dip', 0, 0, tiled=True)  9.89 us
  transfers between devices with their start and end apart: 1, of which 1 were waited for; matrix products, arithmetic and copies ran while one was open for 0% of the time, Pallas kernels for 2%

profile of v1, /device:TPU:1, one launch (start us, length us, event | category | flops | bytes accessed | tf_op | source)
XLA Modules:
  0.0 154.8 jit_solution(15865966591143988434)
XLA Ops:
  0.6 1.9 %shard_map.131 = f32[4,112,256]{2,1,0:T(8,128)} custom-call(f32[3,64,256]{2,1,0:T(8,128)} %slip.1, f32[2,64,256]{2,1,0:T(8,128)} %prestress.1, f32[64,256]{1,0:T(8,128)} %normal.1, f32[64,256]{1,0:T(8,128)} %effect.1, f32[64,256]{1,0:T(8,128)} %state.1), custom_call_target="tpu_custom_call" | custom-call | tf_op jit(solution)/shard_map/pallas_call | solution.py:300
  2.5 11.5 %all_to_all.30.fields = f32[4,112,256]{2,1,0:T(8,128)} all-to-all(f32[4,112,256]{2,1,0:T(8,128)} %shard_map.131), channel_id=1, replica_groups=mesh['strike'=64,'dip'=4] {'dip'}, dimensions={0} | all-to-all | bytes 917504 | tf_op jit(solution)/shard_map/all_to_all | solution.py:321
  14.0 2.5 %shard_map.132 = f32[768,128]{1,0:T(8,128)} custom-call(f32[4,112,256]{2,1,0:T(8,128)} %all_to_all.30.fields, f32[8,256]{1,0:T(8,128)} %constant.10.clone.turn, bf16[2,512,256]{2,1,0:T(8,128)(2,1)} %constant.11.clone.dft), custom_call_target="tpu_custom_call" | custom-call | tf_op jit(solution)/shard_map/pallas_call | solution.py:300
  16.5 15.5 %all-to-all-start.1 = ((f32[256,1,384]{2,1,0:T(1,128)}), f32[256,1,384]{2,1,0:T(1,128)S(1)}, u32[]{:S(2)}, u32[]{:S(2)}) async-start(f32[256,1,384]{2,1,0:T(1,128)} %bitcast.8), calls=%async_computation.1 | async-start | bytes 786432 | tf_op jit(solution)/shard_map/all_to_all | solution.py:308
  32.0 3.4 %shard_map.133 = (f32[3,128,256]{2,1,0:T(8,128)}, f32[3,128,256]{2,1,0:T(8,128)}, f32[8,64,256]{2,1,0:T(8,128)}) custom-call(bf16[4,3,2,4,4096]{4,3,2,1,0:T(4,128)(2,1)} %history.1, s32[4,4096]{1,0:T(4,128)} %lengths.1), custom_call_target="tpu_custom_call" | custom-call | tf_op jit(solution)/shard_map/pallas_call | solution.py:300
  35.4 15.1 %all-to-all-done.1 = f32[256,1,384]{2,1,0:T(1,128)S(1)} async-done(((f32[256,1,384]{2,1,0:T(1,128)}), f32[256,1,384]{2,1,0:T(1,128)S(1)}, u32[]{:S(2)}, u32[]{:S(2)}) %all-to-all-start.1) | async-done | bytes 393248 | tf_op jit(solution)/shard_map/all_to_all | solution.py:308
  50.5 0.0 copy-start
  50.5 0.8 copy-done
  51.3 4.3 %shard_map.134 = (f32[768,128]{1,0:T(8,128)}, f32[128,768]{1,0:T(8,128)}) custom-call(f32[768,128]{1,0:T(8,128)} %bitcast.10, f32[3,128,256]{2,1,0:T(8,128)} %get-tuple-element.9.past, f32[8,64,256]{2,1,0:T(8,128)} %get-tuple-element.10.coef, f32[2,16,256]{2,1,0:T(8,128)} %constant.12.clone.twist, bf16[2,512,256]{2,1,0:T(8,128)(2,1)} %constant.11.clone.dft, ...), custom_call_target="tpu_custom_call" | custom-call | tf_op jit(solution)/shard_map/pallas_call | solution.py:300
  55.5 25.6 %all_to_all.31 = f32[256,1,384]{2,1,0:T(1,128)} all-to-all(f32[256,1,384]{2,1,0:T(1,128)} %bitcast.14), channel_id=1, replica_groups=mesh['strike'=64,'dip'=4] {'strike','dip'}, dimensions={0} | all-to-all | bytes 786432 | tf_op jit(solution)/shard_map/all_to_all | solution.py:308
  81.1 3.8 %shard_map.135 = (f32[768,128]{1,0:T(8,128)}, f32[64,256]{1,0:T(8,128)}) custom-call(f32[768,128]{1,0:T(8,128)} %bitcast.9, f32[4,112,256]{2,1,0:T(8,128)} %all_to_all.30.fields, f32[8,256]{1,0:T(8,128)} %constant.10.clone.turn, bf16[2,512,256]{2,1,0:T(8,128)(2,1)} %constant.11.clone.dft), custom_call_target="tpu_custom_call" | custom-call | tf_op jit(solution)/shard_map/pallas_call | solution.py:300
  85.0 25.6 %all_to_all.32 = f32[256,1,384]{2,1,0:T(1,128)} all-to-all(f32[256,1,384]{2,1,0:T(1,128)} %bitcast.15), channel_id=1, replica_groups=mesh['strike'=64,'dip'=4] {'strike','dip'}, dimensions={0} | all-to-all | bytes 786432 | tf_op jit(solution)/shard_map/all_to_all | solution.py:308
  110.6 4.3 %shard_map.136 = f32[768,128]{1,0:T(8,128)} custom-call(f32[768,128]{1,0:T(8,128)} %bitcast.11, f32[3,128,256]{2,1,0:T(8,128)} %get-tuple-element.13.past, f32[8,64,256]{2,1,0:T(8,128)} %get-tuple-element.10.coef, f32[128,768]{1,0:T(8,128)} %get-tuple-element.14.older, f32[2,16,256]{2,1,0:T(8,128)} %constant.12.clone.twist, ...), custom_call_target="tpu_custom_call" | custom-call | tf_op jit(solution)/shard_map/pallas_call | solution.py:300
  114.9 25.6 %all_to_all.33 = f32[256,1,384]{2,1,0:T(1,128)} all-to-all(f32[256,1,384]{2,1,0:T(1,128)} %bitcast.12), channel_id=1, replica_groups=mesh['strike'=64,'dip'=4] {'strike','dip'}, dimensions={0} | all-to-all | bytes 786432 | tf_op jit(solution)/shard_map/all_to_all | solution.py:308
  140.5 2.8 %shard_map.137 = f32[4,64,256]{2,1,0:T(8,128)} custom-call(f32[768,128]{1,0:T(8,128)} %bitcast.13, f32[4,112,256]{2,1,0:T(8,128)} %all_to_all.30.fields, f32[64,256]{1,0:T(8,128)} %get-tuple-element.15.state_in, f32[8,256]{1,0:T(8,128)} %constant.10.clone.turn, bf16[2,512,256]{2,1,0:T(8,128)(2,1)} %constant.11.clone.dft), custom_call_target="tpu_custom_call" | custom-call | tf_op jit(solution)/shard_map/pallas_call | solution.py:300
  143.3 9.9 %all_to_all.34.gathered = f32[4,64,256]{2,1,0:T(8,128)} all-to-all(f32[4,64,256]{2,1,0:T(8,128)} %shard_map.137), channel_id=1, replica_groups=mesh['strike'=64,'dip'=4] {'dip'}, dimensions={0} | all-to-all | bytes 524288 | tf_op jit(solution)/shard_map/all_to_all | solution.py:340
  153.2 1.7 %shard_map.138 = (f32[3,64,256]{2,1,0:T(8,128)}, f32[64,256]{1,0:T(8,128)}) custom-call(f32[4,64,256]{2,1,0:T(8,128)} %all_to_all.34.gathered), custom_call_target="tpu_custom_call" | custom-call | tf_op jit(solution)/shard_map/pallas_call | solution.py:300
Async XLA Ops:
  16.5 34.0 %all-to-all-start.1 = ((f32[256,1,384]{2,1,0:T(1,128)}), f32[256,1,384]{2,1,0:T(1,128)S(1)}, u32[]{:S(2)}, u32[]{:S(2)}) async-start(f32[256,1,384]{2,1,0:T(1,128)} %bitcast.8), calls=%async_computation.1 | async-start | bytes 786432 | tf_op jit(solution)/shard_map/all_to_all | solution.py:308
  50.5 0.8 copy-start

commit v2 on v1

--- a/solution.py
+++ b/solution.py
@@ -296,11 +296,12 @@
     lines_of(out, force, twist, dft, back)
 
 
-def call(kernel, outs, *args, scratch=()):
+def call(kernel, outs, *args, scratch=(), grant=20):
     return pl.pallas_call(
         kernel,
         out_shape=[jax.ShapeDtypeStruct(s, F32) for s in outs],
         scratch_shapes=scratch,
+        compiler_params=pltpu.CompilerParams(vmem_limit_bytes=grant << 20),
     )(*args)
 
 
@@ -316,7 +317,14 @@
     lines = (768, 128)
 
     (packed,) = call(
-        pack_kernel, [(4, 112, 256)], slip_rate, prestress, normal_stress, direct_effect, state_log
+        pack_kernel,
+        [(4, 112, 256)],
+        slip_rate,
+        prestress,
+        normal_stress,
+        direct_effect,
+        state_log,
+        grant=60,
     )
     fields = lax.all_to_all(packed, "dip", 0, 0, tiled=True)
     past1, past2, coef = call(

time: 155 us -> 139 us (0.90)
  Pallas kernels: 24.6 us -> 11.9 us
  blocking collectives: 98.2 us -> 91.9 us
  local copies, waits for them, and re-layouts: 0.75 us -> 2.45 us
    pallas_call x8, Pallas kernels: 24.6 us -> 11.9 us  [call(): pl.pallas_call(kernel, out_shape=[jax.ShapeDtypeStruct(s, F32) for s in o...]
    all_to_all x3, blocking collectives: 76.8 us -> 72 us  [exchange(): lax.all_to_all(lines.reshape(DEV, 1, 384), BOTH, 0, 0, tiled=True)]
    all_to_all x1, blocking collectives: 9.89 us -> 8.14 us  [shards(): gathered = lax.all_to_all(out, 'dip', 0, 0, tiled=True)]
    unnamed x2 -> x14, local copies, waits for them, and re-layouts: 0.75 us -> 2.45 us
  transfers between devices with their start and end apart: 1 -> 1, of which waited for: 1 -> 1; matrix products, arithmetic and copies ran while one was open for 0% -> 0% of each run, Pallas kernels for 2% -> 1%
where the time goes in v2:
time: 139 us; the launch traced here: 138 us
  blocking collectives  91.9 us (66%)
  waiting for transfers between devices  16.1 us (12%)
  starting transfers between devices  15.3 us (11%)
  Pallas kernels  11.9 us (9%)
  local copies, waits for them, and re-layouts  2.45 us (2%)
    all_to_all x3, blocking collectives, exchange(): lax.all_to_all(lines.reshape(DEV, 1, 384), BOTH, 0, 0, tiled=True)  72 us
    all_to_all x1, waiting for transfers between devices, exchange(): lax.all_to_all(lines.reshape(DEV, 1, 384), BOTH, 0, 0, tiled=True)  16.1 us
    all_to_all x1, starting transfers between devices, exchange(): lax.all_to_all(lines.reshape(DEV, 1, 384), BOTH, 0, 0, tiled=True)  15.3 us
    pallas_call x8, Pallas kernels, call(): pl.pallas_call(kernel, out_shape=[jax.ShapeDtypeStruct(s, F32) for s in o...  11.9 us
    all_to_all x1, blocking collectives, shards(): fields = lax.all_to_all(packed, 'dip', 0, 0, tiled=True)  11.7 us
    all_to_all x1, blocking collectives, shards(): gathered = lax.all_to_all(out, 'dip', 0, 0, tiled=True)  8.14 us
  transfers between devices with their start and end apart: 1, of which 1 were waited for; matrix products, arithmetic and copies ran while one was open for 0% of the time, Pallas kernels for 1%

profile of v2, /device:TPU:1, one launch (start us, length us, event | category | flops | bytes accessed | tf_op | source)
XLA Modules:
  0.0 138.3 jit_solution(8318136668216843848)
XLA Ops:
  0.6 1.9 %shard_map.131 = f32[4,112,256]{2,1,0:T(8,128)} custom-call(f32[3,64,256]{2,1,0:T(8,128)} %slip.1, f32[2,64,256]{2,1,0:T(8,128)} %prestress.1, f32[64,256]{1,0:T(8,128)} %normal.1, f32[64,256]{1,0:T(8,128)} %effect.1, f32[64,256]{1,0:T(8,128)} %state.1), custom_call_target="tpu_custom_call" | custom-call | tf_op jit(solution)/shard_map/pallas_call | solution.py:300
  2.5 0.0 copy-start
  2.5 11.7 %all_to_all.30.fields = f32[4,112,256]{2,1,0:T(8,128)S(1)} all-to-all(f32[4,112,256]{2,1,0:T(8,128)} %shard_map.131), channel_id=1, replica_groups=mesh['strike'=64,'dip'=4] {'dip'}, dimensions={0} | all-to-all | bytes 917504 | tf_op jit(solution)/shard_map/all_to_all | solution.py:329
  14.2 0.0 copy-done
  14.2 0.0 copy-done.5
  14.2 1.3 shard_map.132
  15.5 15.3 %all-to-all-start.1 = ((f32[256,1,384]{2,1,0:T(1,128)}), f32[256,1,384]{2,1,0:T(1,128)S(1)}, u32[]{:S(2)}, u32[]{:S(2)}) async-start(f32[256,1,384]{2,1,0:T(1,128)} %bitcast), calls=%async_computation.1 | async-start | bytes 786432 | tf_op jit(solution)/shard_map/all_to_all | solution.py:309
  30.8 0.0 copy-done.1
  30.8 0.0 copy-start.6
  30.8 0.8 copy-done.6
  31.6 1.5 %shard_map.133 = (f32[3,128,256]{2,1,0:T(8,128)S(1)}, f32[3,128,256]{2,1,0:T(8,128)S(1)}, f32[8,64,256]{2,1,0:T(8,128)S(1)}) custom-call(bf16[4,3,2,4,4096]{4,3,2,1,0:T(4,128)(2,1)S(1)} %copy-done.1, s32[4,4096]{1,0:T(4,128)S(1)} %copy-done.6), custom_call_target="tpu_custom_call" | custom-call | tf_op jit(solution)/shard_map/pallas_call | solution.py:300
  33.2 16.1 %all-to-all-done.1 = f32[256,1,384]{2,1,0:T(1,128)S(1)} async-done(((f32[256,1,384]{2,1,0:T(1,128)}), f32[256,1,384]{2,1,0:T(1,128)S(1)}, u32[]{:S(2)}, u32[]{:S(2)}) %all-to-all-start.1) | async-done | bytes 393248 | tf_op jit(solution)/shard_map/all_to_all | solution.py:309
  49.3 0.0 copy-done.2
  49.3 0.8 copy-done.3
  50.1 0.8 copy-done.4
  50.9 2.0 %shard_map.134 = (f32[768,128]{1,0:T(8,128)S(1)}, f32[128,768]{1,0:T(8,128)S(1)}) custom-call(f32[768,128]{1,0:T(8,128)S(1)} %bitcast.9, f32[3,128,256]{2,1,0:T(8,128)S(1)} %get-tuple-element.9.past, f32[8,64,256]{2,1,0:T(8,128)S(1)} %get-tuple-element.10.coef, f32[2,16,256]{2,1,0:T(8,128)S(1)} %copy-done.4, bf16[2,512,256]{2,1,0:T(8,128)(2,1)S(1)} %copy-done, ...), custom_call_target="tpu_custom_call" | custom-call | tf_op jit(solution)/shard_map/pallas_call | solution.py:300
  52.9 24.0 %all_to_all.31 = f32[256,1,384]{2,1,0:T(1,128)S(1)} all-to-all(f32[256,1,384]{2,1,0:T(1,128)S(1)} %bitcast.13), channel_id=1, replica_groups=mesh['strike'=64,'dip'=4] {'strike','dip'}, dimensions={0} | all-to-all | bytes 786432 | tf_op jit(solution)/shard_map/all_to_all | solution.py:309
  76.9 1.8 %shard_map.135 = (f32[768,128]{1,0:T(8,128)S(1)}, f32[64,256]{1,0:T(8,128)S(1)}) custom-call(f32[768,128]{1,0:T(8,128)S(1)} %bitcast.8, f32[4,112,256]{2,1,0:T(8,128)S(1)} %all_to_all.30.fields, f32[8,256]{1,0:T(8,128)S(1)} %copy-done.5, bf16[2,512,256]{2,1,0:T(8,128)(2,1)S(1)} %copy-done), custom_call_target="tpu_custom_call" | custom-call | tf_op jit(solution)/shard_map/pallas_call | solution.py:300
  78.6 24.0 %all_to_all.32 = f32[256,1,384]{2,1,0:T(1,128)S(1)} all-to-all(f32[256,1,384]{2,1,0:T(1,128)S(1)} %bitcast.14), channel_id=1, replica_groups=mesh['strike'=64,'dip'=4] {'strike','dip'}, dimensions={0} | all-to-all | bytes 786432 | tf_op jit(solution)/shard_map/all_to_all | solution.py:309
  102.7 2.1 %shard_map.136 = f32[768,128]{1,0:T(8,128)S(1)} custom-call(f32[768,128]{1,0:T(8,128)S(1)} %bitcast.10, f32[3,128,256]{2,1,0:T(8,128)S(1)} %get-tuple-element.13.past, f32[8,64,256]{2,1,0:T(8,128)S(1)} %get-tuple-element.10.coef, f32[128,768]{1,0:T(8,128)S(1)} %get-tuple-element.14.older, f32[2,16,256]{2,1,0:T(8,128)S(1)} %copy-done.4, ...), custom_call_target="tpu_custom_call" | custom-call | tf_op jit(solution)/shard_map/pallas_call | solution.py:300
  104.7 24.0 %all_to_all.33 = f32[256,1,384]{2,1,0:T(1,128)S(1)} all-to-all(f32[256,1,384]{2,1,0:T(1,128)S(1)} %bitcast.11), channel_id=1, replica_groups=mesh['strike'=64,'dip'=4] {'strike','dip'}, dimensions={0} | all-to-all | bytes 786432 | tf_op jit(solution)/shard_map/all_to_all | solution.py:309
  128.8 0.7 shard_map.137
  129.5 8.1 %all_to_all.34.gathered = f32[4,64,256]{2,1,0:T(8,128)S(1)} all-to-all(f32[4,64,256]{2,1,0:T(8,128)S(1)} %shard_map.137), channel_id=1, replica_groups=mesh['strike'=64,'dip'=4] {'dip'}, dimensions={0} | all-to-all | bytes 524288 | tf_op jit(solution)/shard_map/all_to_all | solution.py:348
  137.6 0.7 shard_map.138
  (5 shorter events, 0.0 us)
Async XLA Ops:
  2.5 11.7 %copy-start = (bf16[2,512,256]{2,1,0:T(8,128)(2,1)S(1)}, bf16[2,512,256]{2,1,0:T(8,128)(2,1)}, u32[]{:S(2)}) copy-start(bf16[2,512,256]{2,1,0:T(8,128)(2,1)} %constant.11.clone.dft) | copy-start | bytes 1572868
  2.5 11.7 %copy-start.5 = (f32[8,256]{1,0:T(8,128)S(1)}, f32[8,256]{1,0:T(8,128)}, u32[]{:S(2)}) copy-start(f32[8,256]{1,0:T(8,128)} %constant.10.clone.turn) | copy-start | bytes 24580
  14.2 16.6 %copy-start.1 = (bf16[4,3,2,4,4096]{4,3,2,1,0:T(4,128)(2,1)S(1)}, bf16[4,3,2,4,4096]{4,3,2,1,0:T(4,128)(2,1)}, u32[]{:S(2)}) copy-start(bf16[4,3,2,4,4096]{4,3,2,1,0:T(4,128)(2,1)} %history.1) | copy-start | bytes 2359300
  15.5 33.7 %all-to-all-start.1 = ((f32[256,1,384]{2,1,0:T(1,128)}), f32[256,1,384]{2,1,0:T(1,128)S(1)}, u32[]{:S(2)}, u32[]{:S(2)}) async-start(f32[256,1,384]{2,1,0:T(1,128)} %bitcast), calls=%async_computation.1 | async-start | bytes 786432 | tf_op jit(solution)/shard_map/all_to_all | solution.py:309
  30.8 0.8 copy-start.6
  31.6 17.6 %copy-start.2 = (bf16[2,128,128]{2,1,0:T(8,128)(2,1)S(1)}, bf16[2,128,128]{2,1,0:T(8,128)(2,1)}, u32[]{:S(2)}) copy-start(bf16[2,128,128]{2,1,0:T(8,128)(2,1)} %constant.14.clone.back) | copy-start | bytes 196612
  49.3 0.8 copy-start.3
  50.1 0.8 copy-start.4

commit v3 on v2

v3 whole, which is shorter than its diff:
```python
import math

import jax
import jax.numpy as jnp
import numpy as np
from jax import lax
from jax.experimental import pallas as pl
from jax.experimental.pallas import tpu as pltpu
from jax.sharding import PartitionSpec as P

NX, NZ = 4096, 1024
DEV = 256
ROWS = NX // DEV
MODES = NZ // DEV
NEWTON = 2
BOTH = ("strike", "dip")
F32, BF16 = jnp.float32, jnp.bfloat16


def split(value):
    high = value.astype(BF16)
    low = (value - high.astype(F32)).astype(BF16)
    return high, low


def split_table(table):
    table = np.asarray(table, np.float64)
    high = table.astype(np.float32).astype(jnp.bfloat16)
    low = (table - high.astype(np.float64)).astype(np.float32).astype(jnp.bfloat16)
    return np.stack([high, low])


def dft_table():
    index = np.arange(DEV)
    angle = 2 * np.pi * (np.outer(index, index) % DEV) / DEV
    return split_table(np.concatenate([np.cos(angle), np.sin(angle)], 0))


def inner_table(sign):
    angle = 2 * np.pi * (np.outer(np.arange(ROWS), np.arange(ROWS)) % ROWS) / ROWS
    cos, sin = np.cos(angle) / math.sqrt(NX), sign * np.sin(angle) / math.sqrt(NX)
    table = np.zeros((2, ROWS, MODES, 2, MODES, ROWS))
    for m in range(MODES):
        table[0, :, m, 0, m, :] = cos
        table[0, :, m, 1, m, :] = -sin
        table[1, :, m, 0, m, :] = sin
        table[1, :, m, 1, m, :] = cos
    return table.reshape(128, 128)


def inverse_inner():
    forward = inner_table(-1.0).reshape(2, ROWS, MODES, 2, MODES, ROWS)
    return forward.transpose(3, 4, 5, 0, 1, 2).reshape(128, 128)


def twist_table():
    angle = 2 * np.pi * np.outer(np.arange(ROWS), np.arange(DEV)) / NX
    return np.concatenate([np.cos(angle), np.sin(angle)]).astype(np.float32)


def turn_table():
    angle = 2 * np.pi * np.outer(np.arange(MODES), np.arange(DEV)) / NZ
    table = np.stack([np.cos(angle), np.sin(angle)]) / math.sqrt(NZ)
    return table.reshape(2 * MODES, DEV).astype(np.float32)


def matrix_tables():
    dft = dft_table().reshape(4 * DEV, DEV)
    sides = [split_table(t) for t in (inner_table(-1.0), inverse_inner())]
    return np.concatenate([dft] + [np.concatenate([t[0], t[1]], 1) for t in sides], 0)


def angle_tables():
    return np.concatenate([twist_table(), turn_table()], 0)


def dot3(left, right):
    lh, ll = left
    rh, rl = right
    out = jnp.dot(lh, rh, preferred_element_type=F32)
    out += jnp.dot(ll, rh, preferred_element_type=F32)
    out += jnp.dot(lh, rl, preferred_element_type=F32)
    return out


def long_dft(blocks, mats, sign):
    rows = []
    for real, imag in blocks:
        if sign < 0:
            rows.append(jnp.concatenate([real, imag], 1))
            rows.append(jnp.concatenate([imag, -real], 1))
        else:
            rows.append(jnp.concatenate([real, -imag], 1))
            rows.append(jnp.concatenate([imag, real], 1))
    table = (mats[: 2 * DEV, :], mats[2 * DEV : 4 * DEV, :])
    out = dot3(split(jnp.concatenate(rows, 0)), table)
    return [
        (out[128 * c : 128 * c + 64], out[128 * c + 64 : 128 * c + 128])
        for c in range(len(blocks))
    ]


def read_lines(ref, which, count):
    blocks = []
    for c in which:
        lines = ref[pl.ds(c, DEV, stride=count), :].T
        blocks.append((lines[:64], lines[64:]))
    return blocks


def write_lines(ref, blocks):
    for c, (real, imag) in enumerate(blocks):
        ref[pl.ds(c, DEV, stride=len(blocks)), :] = jnp.concatenate([real, imag], 0).T


def turns(angles):
    cos = [angles[32 + m : 33 + m, :] for m in range(4)]
    sin = [angles[36 + m : 37 + m, :] for m in range(4)]
    return cos, sin


def dip_forward(field, angles):
    cos, sin = turns(angles)
    blocks = []
    for x0, x1, x2, x3 in field:
        even, odd, f, g = x0 + x2, x1 + x3, x0 - x2, x1 - x3
        y0, y2 = even + odd, even - odd
        real = [y0 * cos[0], f * cos[1] - g * sin[1], y2 * cos[2], f * cos[3] + g * sin[3]]
        imag = [
            jnp.zeros_like(y0),
            -(f * sin[1] + g * cos[1]),
            -(y2 * sin[2]),
            g * cos[3] - f * sin[3],
        ]
        blocks.append((jnp.concatenate(real, 0), jnp.concatenate(imag, 0)))
    return blocks


def dip_inverse(blocks, angles):
    cos, sin = turns(angles)
    field = []
    for real, imag in blocks:
        re = [real[16 * m : 16 * m + 16] for m in range(4)]
        im = [imag[16 * m : 16 * m + 16] for m in range(4)]
        u = [cos[m] * re[m] - sin[m] * im[m] for m in range(4)]
        v1 = cos[1] * im[1] + sin[1] * re[1]
        v3 = cos[3] * im[3] + sin[3] * re[3]
        a, b, c, d = u[0] + u[2], u[0] - u[2], u[1] + u[3], v3 - v1
        field.append(jnp.concatenate([a + c, b + d, a - c, b - d], 0))
    return field


def friction(force, prestress, strength, state):
    load_strike = prestress[0] + force[0]
    load_dip = prestress[1] + force[1]
    traction = jnp.sqrt(load_strike * load_strike + load_dip * load_dip)
    factor = jnp.exp(-state)
    ratio = traction / factor
    estimate = jnp.minimum(traction / strength, jnp.log(ratio + jnp.sqrt(ratio * ratio + 1.0)))
    half = 0.5 * factor
    for _ in range(NEWTON):
        up, down = jnp.exp(estimate), jnp.exp(-estimate)
        residual = traction - strength * estimate - half * (up - down)
        estimate = estimate + residual / (strength + half * (up + down))
    slip_speed = 2.0 * (traction - strength * estimate)
    scale = slip_speed / jnp.maximum(traction, 1.0)
    rates = [scale * load_strike, scale * load_dip]
    return rates, state + 0.5 * (factor - 0.5 * slip_speed)


def pack_slip_kernel(slip, out):
    for d in range(4):
        for c in range(3):
            out[d, 16 * c : 16 * c + 16, :] = slip[c, 16 * d : 16 * d + 16, :]


def pack_rest_kernel(prestress, normal, effect, state, *outs):
    own = lax.axis_index("dip")
    for i, out in enumerate(outs):
        rows = pl.ds(pl.multiple_of(lax.rem(own + i, 4) * 16, 16), 16)
        for c in range(2):
            out[16 * c : 16 * c + 16, :] = prestress[c, rows, :]
        out[32:48, :] = normal[rows, :] * effect[rows, :]
        out[48:64, :] = state[rows, :]


def first_kernel(fields, angles, mats, out):
    field = [[fields[d, 16 * c : 16 * c + 16, :] for d in range(4)] for c in range(3)]
    write_lines(out, long_dft(dip_forward(field, angles), mats, -1))


def middle_kernel(lines, part0, part1, part2, part3, angles, mats, out, state_out, fields):
    own = lax.axis_index("dip")
    for i, part in enumerate((part0, part1, part2, part3)):
        rows = pl.ds(pl.multiple_of(lax.rem(own + 4 - i, 4) * 16, 16), 16)
        for c in range(3):
            fields[c, rows, :] = part[16 * c : 16 * c + 16, :]
        state_out[rows, :] = part[48:64, :]
    force = dip_inverse(long_dft(read_lines(lines, (0, 1), 3), mats, 1), angles)
    rates, state = friction(force, (fields[0], fields[1]), fields[2], state_out[...])
    state_out[...] = state
    field = [[r[16 * d : 16 * d + 16] for d in range(4)] for r in rates]
    write_lines(out, long_dft(dip_forward(field, angles), mats, -1))


def opening_kernel(lines, angles, mats, out):
    out[...] = 2.0 * dip_inverse(long_dft(read_lines(lines, (2,), 3), mats, 1), angles)[0]


def last_kernel(lines, fields, state_in, opening, angles, mats, out):
    force = dip_inverse(long_dft(read_lines(lines, (0, 1), 2), mats, 1), angles)
    rates, state = friction(force, (fields[0], fields[1]), fields[2], state_in[...])
    for d in range(4):
        for c, value in enumerate(rates + [opening, state]):
            out[d, 16 * c : 16 * c + 16, :] = value[16 * d : 16 * d + 16, :]


def unpack_kernel(gathered, rates, state):
    for d in range(4):
        rows = slice(16 * d, 16 * d + 16)
        for c in range(3):
            rates[c, rows, :] = gathered[d, 16 * c : 16 * c + 16, :]
        state[rows, :] = gathered[d, 48:64, :]


def mixing(device):
    shape = (64, DEV)
    row = lax.broadcasted_iota(jnp.int32, shape, 0)
    kx = (row >> 2) * DEV + lax.broadcasted_iota(jnp.int32, shape, 1)
    kz = device * MODES + (row & 3)
    mz = jnp.where(2 * kz < NZ, kz, kz - NZ)
    mx = jnp.where(2 * kx < NX, kx, kx - NX)
    qz = mz.astype(F32) * (2.0 * math.pi / NZ)
    qx = mx.astype(F32) * (2.0 * math.pi / NX)
    q = jnp.sqrt(qx * qx + qz * qz)
    anchor = (mz == 0) & (mx == 0)
    safe = jnp.where(anchor, 1.0, q)
    ex = jnp.where(anchor, 1.0, qx / safe)
    ez = jnp.where(anchor, 0.0, qz / safe)
    xx, xz, zz = ex * ex, ex * ez, ez * ez
    decay = jnp.exp(-0.025 * q)
    envelope = -0.25 * q
    first = [jnp.cos(0.5 * s * q) for s in (1.0, 0.6, 1.7)]
    before = [jnp.ones(shape, F32)] * 3
    now = first
    out = []
    for lag in range(4):
        envelope = envelope * decay
        two, three, one = [envelope * c for c in now]
        out.append((xx * two + zz * three, xz * (two - three), zz * two + xx * three, one))
        now, before = [2.0 * f * c - p for f, c, p in zip(first, now, before)], now
    return out


def history_kernel(history, lengths, past1, past2, coef, held, reach):
    device = lax.axis_index("strike") * 4 + lax.axis_index("dip")
    for k1 in range(16):
        lanes = slice(DEV * k1, DEV * k1 + DEV)
        rows = slice(4 * k1, 4 * k1 + 4)
        reach[rows, :] = lengths[:, lanes].astype(F32)
    for lag in range(3):
        for c in range(3):
            for part in range(2):
                line = history[lag, c, part].astype(F32)
                for k1 in range(16):
                    held[lag, c, part, 4 * k1 : 4 * k1 + 4, :] = line[:, DEV * k1 : DEV * k1 + DEV]
    mix = mixing(device)
    length = reach[...]
    masked = [None] + [
        [jnp.where(length > float(lag), m, 0.0) for m in mix[lag]] for lag in range(1, 4)
    ]
    twice = 2.0 * mix[0][3]
    for i in range(3):
        coef[i] = mix[0][i]
        coef[4 + i] = masked[1][i]
    coef[3] = twice * mix[0][3] + masked[1][3]
    for part in range(2):
        rows = slice(64 * part, 64 * part + 64)
        totals = []
        for skip in (1, 2):
            total = [0.0, 0.0, 0.0]
            for lag in range(skip, 4):
                ss, sd, dd, op = masked[lag]
                a, b, c = [held[lag - skip, i, part] for i in range(3)]
                total[0] = total[0] + (ss * a + sd * b)
                total[1] = total[1] + (sd * a + dd * b)
                total[2] = total[2] + op * c
            totals.append(total)
        for i in range(2):
            past1[i, rows, :] = totals[0][i]
            past2[i, rows, :] = totals[1][i]
        past1[2, rows, :] = twice * totals[0][2] + totals[1][2]


def spectrum_of(blocks, angles, mats):
    blocks = long_dft(blocks, mats, -1)
    cos = jnp.concatenate([angles[0:16, :]] * 4, 0)
    sin = jnp.concatenate([angles[16:32, :]] * 4, 0)
    turned = [
        jnp.concatenate([re * cos + im * sin, im * cos - re * sin], 0) for re, im in blocks
    ]
    inner = (mats[1024:1152, :128], mats[1024:1152, 128:])
    return dot3(inner, split(jnp.concatenate(turned, 1)))


def lines_of(out, force, angles, mats):
    back = (mats[1152:1280, :128], mats[1152:1280, 128:])
    blocks = dot3(back, split(jnp.concatenate(force, 1)))
    cos = jnp.concatenate([angles[0:16, :]] * 4, 0)
    sin = jnp.concatenate([angles[16:32, :]] * 4, 0)
    turned = []
    for c in range(len(force)):
        re, im = blocks[:64, DEV * c : DEV * c + DEV], blocks[64:, DEV * c : DEV * c + DEV]
        turned.append((re * cos - im * sin, im * cos + re * sin))
    write_lines(out, long_dft(turned, mats, 1))


def both_parts(coef, i):
    return jnp.concatenate([coef[i]] * 2, 0)


def apply_mix(coef, at, spec):
    ss, sd, dd = [both_parts(coef, at + i) for i in range(3)]
    s, d = spec[:, :DEV], spec[:, DEV : 2 * DEV]
    return [ss * s + sd * d, sd * s + dd * d]


def mode_kernel_first(lines, past, coef, angles, mats, out, spec_out):
    spec = spectrum_of(read_lines(lines, (0, 1, 2), 3), angles, mats)
    spec_out[...] = spec[:, : 2 * DEV]
    force = apply_mix(coef, 0, spec) + [both_parts(coef, 3) * spec[:, 2 * DEV :]]
    lines_of(out, [f + past[c] for c, f in enumerate(force)], angles, mats)


def older_kernel(past, coef, spec, out):
    for c, f in enumerate(apply_mix(coef, 4, spec)):
        out[c] = f + past[c]


def mode_kernel_second(lines, older, coef, angles, mats, out):
    spec = spectrum_of(read_lines(lines, (0, 1), 2), angles, mats)
    force = apply_mix(coef, 0, spec)
    lines_of(out, [f + older[c] for c, f in enumerate(force)], angles, mats)


def call(kernel, outs, *args, scratch=(), grant=20, work=2.0):
    return pl.pallas_call(
        kernel,
        out_shape=[jax.ShapeDtypeStruct(s, F32) for s in outs],
        scratch_shapes=scratch,
        compiler_params=pltpu.CompilerParams(vmem_limit_bytes=grant << 20),
        cost_estimate=pl.CostEstimate(
            flops=int(work * 1e9), bytes_accessed=int(work * 3e6), transcendentals=0
        ),
    )(*args)


def exchange(lines):
    lanes = lines.shape[0] // DEV * 128
    swapped = lax.all_to_all(lines.reshape(DEV, 1, lanes), BOTH, 0, 0, tiled=True)
    return swapped.reshape(lines.shape)


def shards(slip_rate, history, lengths, prestress, normal_stress, direct_effect, state_log):
    mats, angles = matrix_tables(), angle_tables()
    three, two = (3 * DEV, 128), (2 * DEV, 128)
    (packed,) = call(pack_slip_kernel, [(4, 48, 256)], slip_rate, grant=60)
    slip = lax.all_to_all(packed, "dip", 0, 0, tiled=True)
    (out,) = call(first_kernel, [three], slip, angles, mats)
    lines = exchange(out)
    parts = call(
        pack_rest_kernel,
        [(64, 256)] * 4,
        prestress,
        normal_stress,
        direct_effect,
        state_log,
    )
    parts = [
        lax.ppermute(part, "dip", [(j, (j + i) % 4) for j in range(4)]) if i else part
        for i, part in enumerate(parts)
    ]
    past1, past2, coef = call(
        history_kernel,
        [(3, 128, 256), (2, 128, 256), (7, 64, 256)],
        history,
        lengths,
        scratch=[pltpu.VMEM((3, 3, 2, 64, 256), F32), pltpu.VMEM((64, 256), F32)],
    )
    out, spec = call(
        mode_kernel_first, [three, (128, 512)], lines, past1, coef, angles, mats
    )
    lines = exchange(out)
    (older,) = call(older_kernel, [(2, 128, 256)], past2, coef, spec)
    out, state, fields = call(
        middle_kernel, [two, (64, 256), (3, 64, 256)], lines, *parts, angles, mats
    )
    (opening,) = call(opening_kernel, [(64, 256)], lines, angles, mats)
    (out,) = call(mode_kernel_second, [two], exchange(out), older, coef, angles, mats)
    (out,) = call(
        last_kernel, [(4, 64, 256)], exchange(out), fields, state, opening, angles, mats
    )
    gathered = lax.all_to_all(out, "dip", 0, 0, tiled=True)
    rates, state = call(unpack_kernel, [(3, 64, 256), (64, 256)], gathered)
    return rates, state


def solution(mesh):
    return jax.shard_map(
        shards,
        mesh=mesh,
        in_specs=(
            P(None, "strike", "dip"),
            P(None, None, None, ("strike", "dip"), None),
            P(("strike", "dip"), None),
            P(None, "strike", "dip"),
            P("strike", "dip"),
            P("strike", "dip"),
            P("strike", "dip"),
        ),
        out_specs=(P(None, "strike", "dip"), P("strike", "dip")),
        check_vma=False,
    )
```

time: 139 us -> 131 us (0.942)
  blocking collectives: 91.9 us -> 18.3 us
  waiting for transfers between devices: 16.1 us -> 61.7 us
  starting transfers between devices: 15.3 us -> 36.7 us
  local copies, waits for them, and re-layouts: 2.45 us -> 0.03 us
  Pallas kernels: 11.9 us -> 13.4 us
    all_to_all x4 -> x1, blocking collectives: 83.8 us -> 10.1 us  [shards(): slip = lax.all_to_all(packed, 'dip', 0, 0, tiled=True)]
    all_to_all x1 -> x4, waiting for transfers between devices: 16.1 us -> 58.4 us  [exchange(): lax.all_to_all(lines.reshape(DEV, 1, lanes), BOTH, 0, 0, tiled=True)]
    all_to_all x1 -> x4, starting transfers between devices: 15.3 us -> 31.6 us  [exchange(): lax.all_to_all(lines.reshape(DEV, 1, lanes), BOTH, 0, 0, tiled=True)]
    ppermute x0 -> x3, starting transfers between devices: none -> 5.04 us  [shards(): lax.ppermute(part, 'dip', [(j, (j + i) % 4) for j in range(4)])]
    ppermute x0 -> x3, waiting for transfers between devices: none -> 3.31 us  [shards(): lax.ppermute(part, 'dip', [(j, (j + i) % 4) for j in range(4)])]
    unnamed x14 -> x16, local copies, waits for them, and re-layouts: 2.45 us -> 0.03 us
    pallas_call x8 -> x11, Pallas kernels: 11.9 us -> 13.4 us  [call(): pl.pallas_call(kernel, out_shape=[jax.ShapeDtypeStruct(s, F32) for s in o...]
  transfers between devices with their start and end apart: 1 -> 7, of which waited for: 1 -> 5; matrix products, arithmetic and copies ran while one was open for 0% -> 0% of each run, Pallas kernels for 1% -> 1%
where the time goes in v3:
time: 131 us
  waiting for transfers between devices  61.7 us (47%)
  starting transfers between devices  36.7 us (28%)
  blocking collectives  18.3 us (14%)
  Pallas kernels  13.4 us (10%)
    all_to_all x4, waiting for transfers between devices, exchange(): lax.all_to_all(lines.reshape(DEV, 1, lanes), BOTH, 0, 0, tiled=True)  58.4 us
    all_to_all x4, starting transfers between devices, exchange(): lax.all_to_all(lines.reshape(DEV, 1, lanes), BOTH, 0, 0, tiled=True)  31.6 us
    pallas_call x11, Pallas kernels, call(): pl.pallas_call(kernel, out_shape=[jax.ShapeDtypeStruct(s, F32) for s in o...  13.4 us
    all_to_all x1, blocking collectives, shards(): slip = lax.all_to_all(packed, 'dip', 0, 0, tiled=True)  10.1 us
    all_to_all x1, blocking collectives, shards(): gathered = lax.all_to_all(out, 'dip', 0, 0, tiled=True)  8.15 us
    ppermute x3, starting transfers between devices, shards(): lax.ppermute(part, 'dip', [(j, (j + i) % 4) for j in range(4)])  5.04 us
    ppermute x3, waiting for transfers between devices, shards(): lax.ppermute(part, 'dip', [(j, (j + i) % 4) for j in range(4)])  3.31 us
  transfers between devices with their start and end apart: 7, of which 5 were waited for; matrix products, arithmetic and copies ran while one was open for 0% of the time, Pallas kernels for 1%

profile of v3, /device:TPU:1, one launch (start us, length us, event | category | flops | bytes accessed | tf_op | source)
XLA Modules:
  0.0 130.9 jit_solution(11221375169137623418)
XLA Ops:
  0.6 1.7 %shard_map.104 = f32[4,48,256]{2,1,0:T(8,128)} custom-call(f32[3,64,256]{2,1,0:T(8,128)} %slip.1), custom_call_target="tpu_custom_call" | custom-call | flops 2000000000 | bytes 6000000 | tf_op jit(solution)/shard_map/pallas_call | solution.py:347
  2.3 10.1 %all_to_all.30.fields = f32[4,48,256]{2,1,0:T(8,128)S(1)} all-to-all(f32[4,48,256]{2,1,0:T(8,128)} %shard_map.104), channel_id=1, replica_groups=mesh['strike'=64,'dip'=4] {'dip'}, dimensions={0} | all-to-all | bytes 393216 | tf_op jit(solution)/shard_map/all_to_all | solution.py:368
  12.5 1.3 shard_map.105
  13.8 14.4 %all-to-all-start.1 = ((f32[256,1,384]{2,1,0:T(1,128)}), f32[256,1,384]{2,1,0:T(1,128)S(1)}, u32[]{:S(2)}, u32[]{:S(2)}) async-start(f32[256,1,384]{2,1,0:T(1,128)} %bitcast), calls=%async_computation.1 | async-start | bytes 786432 | tf_op jit(solution)/shard_map/all_to_all | solution.py:360
  28.2 1.5 %shard_map.106 = (f32[3,128,256]{2,1,0:T(8,128)S(1)}, f32[2,128,256]{2,1,0:T(8,128)S(1)}, f32[7,64,256]{2,1,0:T(8,128)S(1)}) custom-call(bf16[4,3,2,4,4096]{4,3,2,1,0:T(4,128)(2,1)S(1)} %copy-done, s32[4,4096]{1,0:T(4,128)S(1)} %copy-done.2), custom_call_target="tpu_custom_call" | custom-call | flops 2000000000 | bytes 6000000 | tf_op jit(solution)/shard_map/pallas_call | solution.py:347
  29.7 16.9 %all-to-all-done.1 = f32[256,1,384]{2,1,0:T(1,128)S(1)} async-done(((f32[256,1,384]{2,1,0:T(1,128)}), f32[256,1,384]{2,1,0:T(1,128)S(1)}, u32[]{:S(2)}, u32[]{:S(2)}) %all-to-all-start.1) | async-done | bytes 393248 | tf_op jit(solution)/shard_map/all_to_all | solution.py:360
  46.6 2.8 %shard_map.107 = (f32[768,128]{1,0:T(8,128)}, f32[128,512]{1,0:T(8,128)S(1)}) custom-call(f32[768,128]{1,0:T(8,128)S(1)} %bitcast.10, f32[3,128,256]{2,1,0:T(8,128)S(1)} %get-tuple-element.14.past, f32[7,64,256]{2,1,0:T(8,128)S(1)} %get-tuple-element.15.coef, f32[40,256]{1,0:T(8,128)S(1)} %copy-done.7, bf16[1280,256]{1,0:T(8,128)(2,1)S(1)} %copy-done.6), custom_call_target="tpu_custom_call" | custom-call | flops 2000000000 | bytes 6000000 | tf_op jit(solution)/shard_map/pallas_call | solution.py:347
  49.4 5.8 %all-to-all-start.2 = ((f32[256,1,384]{2,1,0:T(1,128)}), f32[256,1,384]{2,1,0:T(1,128)S(1)}, u32[]{:S(2)}, u32[]{:S(2)}) async-start(f32[256,1,384]{2,1,0:T(1,128)} %bitcast.2), calls=%async_computation.2 | async-start | bytes 786432 | tf_op jit(solution)/shard_map/all_to_all | solution.py:360
  55.3 1.4 %collective-permute-start = (f32[64,256]{1,0:T(8,128)S(1)}, f32[64,256]{1,0:T(8,128)S(1)}, u32[]{:S(2)}, u32[]{:S(2)}) collective-permute-start(f32[64,256]{1,0:T(8,128)S(1)} %get-tuple-element.18), channel_id=1, source_target_pairs={{0,1},{1,2},{2,3},{3,0},{4,5},{5,6},{6,7},{7,4},{8,9},{9,10},{10,1... | collective-permute-start | bytes 196616 | tf_op jit(solution)/shard_map/ppermute | solution.py:380
  56.8 2.4 %collective-permute-start.1 = (f32[64,256]{1,0:T(8,128)S(1)}, f32[64,256]{1,0:T(8,128)S(1)}, u32[]{:S(2)}, u32[]{:S(2)}) collective-permute-start(f32[64,256]{1,0:T(8,128)S(1)} %get-tuple-element.19), channel_id=1, source_target_pairs={{0,2},{1,3},{2,0},{3,1},{4,6},{5,7},{6,4},{7,5},{8,10},{9,11},{10,... | collective-permute-start | bytes 196616 | tf_op jit(solution)/shard_map/ppermute | solution.py:380
  59.2 1.2 collective-permute-start.2
  60.4 3.3 %collective-permute-done.1.part2 = f32[64,256]{1,0:T(8,128)S(1)} collective-permute-done((f32[64,256]{1,0:T(8,128)S(1)}, f32[64,256]{1,0:T(8,128)S(1)}, u32[]{:S(2)}, u32[]{:S(2)}) %collective-permute-start.1) | collective-permute-done | bytes 65568 | tf_op jit(solution)/shard_map/ppermute | solution.py:380
  63.7 10.2 %all-to-all-done.2 = f32[256,1,384]{2,1,0:T(1,128)S(1)} async-done(((f32[256,1,384]{2,1,0:T(1,128)}), f32[256,1,384]{2,1,0:T(1,128)S(1)}, u32[]{:S(2)}, u32[]{:S(2)}) %all-to-all-start.2) | async-done | bytes 393248 | tf_op jit(solution)/shard_map/all_to_all | solution.py:360
  73.9 2.1 %shard_map.109 = (f32[512,128]{1,0:T(8,128)}, f32[64,256]{1,0:T(8,128)S(1)}, f32[3,64,256]{2,1,0:T(8,128)S(1)}) custom-call(f32[768,128]{1,0:T(8,128)S(1)} %bitcast.8, f32[64,256]{1,0:T(8,128)S(1)} %get-tuple-element.17.part0, f32[64,256]{1,0:T(8,128)S(1)} %collective-permute-done.part1, f32[64,256]{1,0:T(8,128)S(1)} %collective-permute-done.1.part2, ...), custom_call_target="tpu_custom_call" | custom-call | flops 2000000000 | bytes 6000000 | tf_op jit(solution)/shard_map/pallas_call | solution.py:347
  76.0 5.7 %all-to-all-start.3 = ((f32[256,1,256]{2,1,0:T(1,128)}), f32[256,1,256]{2,1,0:T(1,128)S(1)}, u32[]{:S(2)}, u32[]{:S(2)}) async-start(f32[256,1,256]{2,1,0:T(1,128)} %bitcast.4), calls=%async_computation.3 | async-start | bytes 524288 | tf_op jit(solution)/shard_map/all_to_all | solution.py:360
  81.7 0.1 shard_map.110.older
  81.7 15.8 %all-to-all-done.3 = f32[256,1,256]{2,1,0:T(1,128)S(1)} async-done(((f32[256,1,256]{2,1,0:T(1,128)}), f32[256,1,256]{2,1,0:T(1,128)S(1)}, u32[]{:S(2)}, u32[]{:S(2)}) %all-to-all-start.3) | async-done | bytes 262176 | tf_op jit(solution)/shard_map/all_to_all | solution.py:360
  97.5 2.3 %shard_map.111 = f32[512,128]{1,0:T(8,128)} custom-call(f32[512,128]{1,0:T(8,128)S(1)} %bitcast.12, f32[2,128,256]{2,1,0:T(8,128)S(1)} %shard_map.110.older, f32[7,64,256]{2,1,0:T(8,128)S(1)} %get-tuple-element.15.coef, f32[40,256]{1,0:T(8,128)S(1)} %copy-done.7, bf16[1280,256]{1,0:T(8,128)(2,1)S(1)} %copy-done.6), custom_call_target="tpu_custom_call" | custom-call | flops 2000000000 | bytes 6000000 | tf_op jit(solution)/shard_map/pallas_call | solution.py:347
  99.8 5.7 %all-to-all-start.4 = ((f32[256,1,256]{2,1,0:T(1,128)}), f32[256,1,256]{2,1,0:T(1,128)S(1)}, u32[]{:S(2)}, u32[]{:S(2)}) async-start(f32[256,1,256]{2,1,0:T(1,128)} %bitcast.6), calls=%async_computation.4 | async-start | bytes 524288 | tf_op jit(solution)/shard_map/all_to_all | solution.py:360
  105.5 0.3 shard_map.112.opening
  105.8 15.5 %all-to-all-done.4 = f32[256,1,256]{2,1,0:T(1,128)S(1)} async-done(((f32[256,1,256]{2,1,0:T(1,128)}), f32[256,1,256]{2,1,0:T(1,128)S(1)}, u32[]{:S(2)}, u32[]{:S(2)}) %all-to-all-start.4) | async-done | bytes 262176 | tf_op jit(solution)/shard_map/all_to_all | solution.py:360
  121.4 0.6 shard_map.113
  122.0 8.2 %all_to_all.31.gathered = f32[4,64,256]{2,1,0:T(8,128)S(1)} all-to-all(f32[4,64,256]{2,1,0:T(8,128)S(1)} %shard_map.113), channel_id=1, replica_groups=mesh['strike'=64,'dip'=4] {'dip'}, dimensions={0} | all-to-all | bytes 524288 | tf_op jit(solution)/shard_map/all_to_all | solution.py:403
  130.2 0.7 shard_map.114
  (19 shorter events, 0.1 us)
Async XLA Ops:
  0.6 11.8 %copy-start.6 = (bf16[1280,256]{1,0:T(8,128)(2,1)S(1)}, bf16[1280,256]{1,0:T(8,128)(2,1)}, u32[]{:S(2)}) copy-start(bf16[1280,256]{1,0:T(8,128)(2,1)} %constant.5.clone.mats) | copy-start | bytes 1966084
  2.3 10.1 %copy-start.7 = (f32[40,256]{1,0:T(8,128)S(1)}, f32[40,256]{1,0:T(8,128)}, u32[]{:S(2)}) copy-start(f32[40,256]{1,0:T(8,128)} %constant.4.clone.angles) | copy-start | bytes 122884
  12.5 15.7 %copy-start.2 = (s32[4,4096]{1,0:T(4,128)S(1)}, s32[4,4096]{1,0:T(4,128)}, u32[]{:S(2)}) copy-start(s32[4,4096]{1,0:T(4,128)} %lengths.1) | copy-start | bytes 196612
  13.8 14.4 %copy-start = (bf16[4,3,2,4,4096]{4,3,2,1,0:T(4,128)(2,1)S(1)}, bf16[4,3,2,4,4096]{4,3,2,1,0:T(4,128)(2,1)}, u32[]{:S(2)}) copy-start(bf16[4,3,2,4,4096]{4,3,2,1,0:T(4,128)(2,1)} %history.1) | copy-start | bytes 2359300
  13.8 32.9 %all-to-all-start.1 = ((f32[256,1,384]{2,1,0:T(1,128)}), f32[256,1,384]{2,1,0:T(1,128)S(1)}, u32[]{:S(2)}, u32[]{:S(2)}) async-start(f32[256,1,384]{2,1,0:T(1,128)} %bitcast), calls=%async_computation.1 | async-start | bytes 786432 | tf_op jit(solution)/shard_map/all_to_all | solution.py:360
  49.4 5.9 %copy-start.1 = (f32[2,64,256]{2,1,0:T(8,128)S(1)}, f32[2,64,256]{2,1,0:T(8,128)}, u32[]{:S(2)}) copy-start(f32[2,64,256]{2,1,0:T(8,128)} %prestress.1) | copy-start | bytes 393220
  49.4 5.9 %copy-start.3 = (f32[64,256]{1,0:T(8,128)S(1)}, f32[64,256]{1,0:T(8,128)}, u32[]{:S(2)}) copy-start(f32[64,256]{1,0:T(8,128)} %normal.1) | copy-start | bytes 196612
  49.4 5.9 %copy-start.4 = (f32[64,256]{1,0:T(8,128)S(1)}, f32[64,256]{1,0:T(8,128)}, u32[]{:S(2)}) copy-start(f32[64,256]{1,0:T(8,128)} %effect.1) | copy-start | bytes 196612
  49.4 5.9 %copy-start.5 = (f32[64,256]{1,0:T(8,128)S(1)}, f32[64,256]{1,0:T(8,128)}, u32[]{:S(2)}) copy-start(f32[64,256]{1,0:T(8,128)} %state.1) | copy-start | bytes 196612
  49.4 24.4 %all-to-all-start.2 = ((f32[256,1,384]{2,1,0:T(1,128)}), f32[256,1,384]{2,1,0:T(1,128)S(1)}, u32[]{:S(2)}, u32[]{:S(2)}) async-start(f32[256,1,384]{2,1,0:T(1,128)} %bitcast.2), calls=%async_computation.2 | async-start | bytes 786432 | tf_op jit(solution)/shard_map/all_to_all | solution.py:360
  55.3 5.0 %collective-permute-start = (f32[64,256]{1,0:T(8,128)S(1)}, f32[64,256]{1,0:T(8,128)S(1)}, u32[]{:S(2)}, u32[]{:S(2)}) collective-permute-start(f32[64,256]{1,0:T(8,128)S(1)} %get-tuple-element.18), channel_id=1, source_target_pairs={{0,1},{1,2},{2,3},{3,0},{4,5},{5,6},{6,7},{7,4},{8,9},{9,10},{10,1... | collective-permute-start | bytes 196616 | tf_op jit(solution)/shard_map/ppermute | solution.py:380
  56.8 6.9 %collective-permute-start.1 = (f32[64,256]{1,0:T(8,128)S(1)}, f32[64,256]{1,0:T(8,128)S(1)}, u32[]{:S(2)}, u32[]{:S(2)}) collective-permute-start(f32[64,256]{1,0:T(8,128)S(1)} %get-tuple-element.19), channel_id=1, source_target_pairs={{0,2},{1,3},{2,0},{3,1},{4,6},{5,7},{6,4},{7,5},{8,10},{9,11},{10,... | collective-permute-start | bytes 196616 | tf_op jit(solution)/shard_map/ppermute | solution.py:380
  59.2 4.5 %collective-permute-start.2 = (f32[64,256]{1,0:T(8,128)S(1)}, f32[64,256]{1,0:T(8,128)S(1)}, u32[]{:S(2)}, u32[]{:S(2)}) collective-permute-start(f32[64,256]{1,0:T(8,128)S(1)} %get-tuple-element.20), channel_id=1, source_target_pairs={{0,3},{1,0},{2,1},{3,2},{4,7},{5,4},{6,5},{7,6},{8,11},{9,8},{10,9... | collective-permute-start | bytes 196616 | tf_op jit(solution)/shard_map/ppermute | solution.py:380
  76.0 21.5 %all-to-all-start.3 = ((f32[256,1,256]{2,1,0:T(1,128)}), f32[256,1,256]{2,1,0:T(1,128)S(1)}, u32[]{:S(2)}, u32[]{:S(2)}) async-start(f32[256,1,256]{2,1,0:T(1,128)} %bitcast.4), calls=%async_computation.3 | async-start | bytes 524288 | tf_op jit(solution)/shard_map/all_to_all | solution.py:360
  99.8 21.6 %all-to-all-start.4 = ((f32[256,1,256]{2,1,0:T(1,128)}), f32[256,1,256]{2,1,0:T(1,128)S(1)}, u32[]{:S(2)}, u32[]{:S(2)}) async-start(f32[256,1,256]{2,1,0:T(1,128)} %bitcast.6), calls=%async_computation.4 | async-start | bytes 524288 | tf_op jit(solution)/shard_map/all_to_all | solution.py:360

commit v4 on v3

--- a/solution.py
+++ b/solution.py
@@ -168,12 +168,6 @@
     return rates, state + 0.5 * (factor - 0.5 * slip_speed)
 
 
-def pack_slip_kernel(slip, out):
-    for d in range(4):
-        for c in range(3):
-            out[d, 16 * c : 16 * c + 16, :] = slip[c, 16 * d : 16 * d + 16, :]
-
-
 def pack_rest_kernel(prestress, normal, effect, state, *outs):
     own = lax.axis_index("dip")
     for i, out in enumerate(outs):
@@ -189,22 +183,19 @@
     write_lines(out, long_dft(dip_forward(field, angles), mats, -1))
 
 
-def middle_kernel(lines, part0, part1, part2, part3, angles, mats, out, state_out, fields):
+def middle_kernel(lines, part0, part1, part2, part3, angles, mats, out, state_out, fields, opening):
     own = lax.axis_index("dip")
     for i, part in enumerate((part0, part1, part2, part3)):
         rows = pl.ds(pl.multiple_of(lax.rem(own + 4 - i, 4) * 16, 16), 16)
         for c in range(3):
             fields[c, rows, :] = part[16 * c : 16 * c + 16, :]
         state_out[rows, :] = part[48:64, :]
-    force = dip_inverse(long_dft(read_lines(lines, (0, 1), 3), mats, 1), angles)
+    force = dip_inverse(long_dft(read_lines(lines, (0, 1, 2), 3), mats, 1), angles)
+    opening[...] = 2.0 * force[2]
     rates, state = friction(force, (fields[0], fields[1]), fields[2], state_out[...])
     state_out[...] = state
     field = [[r[16 * d : 16 * d + 16] for d in range(4)] for r in rates]
     write_lines(out, long_dft(dip_forward(field, angles), mats, -1))
-
-
-def opening_kernel(lines, angles, mats, out):
-    out[...] = 2.0 * dip_inverse(long_dft(read_lines(lines, (2,), 3), mats, 1), angles)[0]
 
 
 def last_kernel(lines, fields, state_in, opening, angles, mats, out):
@@ -325,16 +316,12 @@
     return [ss * s + sd * d, sd * s + dd * d]
 
 
-def mode_kernel_first(lines, past, coef, angles, mats, out, spec_out):
+def mode_kernel_first(lines, past, past_next, coef, angles, mats, out, older):
     spec = spectrum_of(read_lines(lines, (0, 1, 2), 3), angles, mats)
-    spec_out[...] = spec[:, : 2 * DEV]
+    for c, f in enumerate(apply_mix(coef, 4, spec)):
+        older[c] = f + past_next[c]
     force = apply_mix(coef, 0, spec) + [both_parts(coef, 3) * spec[:, 2 * DEV :]]
     lines_of(out, [f + past[c] for c, f in enumerate(force)], angles, mats)
-
-
-def older_kernel(past, coef, spec, out):
-    for c, f in enumerate(apply_mix(coef, 4, spec)):
-        out[c] = f + past[c]
 
 
 def mode_kernel_second(lines, older, coef, angles, mats, out):
@@ -364,7 +351,7 @@
 def shards(slip_rate, history, lengths, prestress, normal_stress, direct_effect, state_log):
     mats, angles = matrix_tables(), angle_tables()
     three, two = (3 * DEV, 128), (2 * DEV, 128)
-    (packed,) = call(pack_slip_kernel, [(4, 48, 256)], slip_rate, grant=60)
+    packed = slip_rate.reshape(3, 4, 16, 256).transpose(1, 0, 2, 3).reshape(4, 48, 256)
     slip = lax.all_to_all(packed, "dip", 0, 0, tiled=True)
     (out,) = call(first_kernel, [three], slip, angles, mats)
     lines = exchange(out)
@@ -387,15 +374,20 @@
         lengths,
         scratch=[pltpu.VMEM((3, 3, 2, 64, 256), F32), pltpu.VMEM((64, 256), F32)],
     )
-    out, spec = call(
-        mode_kernel_first, [three, (128, 512)], lines, past1, coef, angles, mats
-    )
-    lines = exchange(out)
-    (older,) = call(older_kernel, [(2, 128, 256)], past2, coef, spec)
-    out, state, fields = call(
-        middle_kernel, [two, (64, 256), (3, 64, 256)], lines, *parts, angles, mats
-    )
-    (opening,) = call(opening_kernel, [(64, 256)], lines, angles, mats)
+    lines, parts, past1, past2, coef = lax.optimization_barrier(
+        (lines, parts, past1, past2, coef)
+    )
+    out, older = call(
+        mode_kernel_first, [three, (2, 128, 256)], lines, past1, past2, coef, angles, mats
+    )
+    out, state, fields, opening = call(
+        middle_kernel,
+        [two, (64, 256), (3, 64, 256), (64, 256)],
+        exchange(out),
+        *parts,
+        angles,
+        mats,
+    )
     (out,) = call(mode_kernel_second, [two], exchange(out), older, coef, angles, mats)
     (out,) = call(
         last_kernel, [(4, 64, 256)], exchange(out), fields, state, opening, angles, mats

time: 131 us -> 127 us (0.969)
  blocking collectives: 18.3 us -> 84.6 us
  waiting for transfers between devices: 61.7 us -> 11.8 us
  starting transfers between devices: 36.7 us -> 19.4 us
  Pallas kernels: 13.4 us -> 9.34 us
    all_to_all x0 -> x3, blocking collectives: none -> 66.5 us  [exchange(): lax.all_to_all(lines.reshape(DEV, 1, lanes), BOTH, 0, 0, tiled=True)]
    all_to_all x4 -> x1, waiting for transfers between devices: 58.4 us -> 9.98 us  [exchange(): lax.all_to_all(lines.reshape(DEV, 1, lanes), BOTH, 0, 0, tiled=True)]
    all_to_all x4 -> x1, starting transfers between devices: 31.6 us -> 14.4 us  [exchange(): lax.all_to_all(lines.reshape(DEV, 1, lanes), BOTH, 0, 0, tiled=True)]
    pallas_call x11 -> x8, Pallas kernels: 13.4 us -> 9.34 us  [call(): pl.pallas_call(kernel, out_shape=[jax.ShapeDtypeStruct(s, F32) for s in o...]
    ppermute x3, waiting for transfers between devices: 3.31 us -> 1.83 us  [shards(): lax.ppermute(part, 'dip', [(j, (j + i) % 4) for j in range(4)])]
  transfers between devices with their start and end apart: 7 -> 4, of which waited for: 5 -> 2; matrix products, arithmetic and copies ran while one was open for 0% -> 0% of each run, Pallas kernels for 1% -> 1%
where the time goes in v4:
time: 127 us
  blocking collectives  84.6 us (67%)
  starting transfers between devices  19.4 us (15%)
  waiting for transfers between devices  11.8 us (9%)
  Pallas kernels  9.34 us (7%)
    all_to_all x3, blocking collectives, exchange(): lax.all_to_all(lines.reshape(DEV, 1, lanes), BOTH, 0, 0, tiled=True)  66.5 us
    all_to_all x1, starting transfers between devices, exchange(): lax.all_to_all(lines.reshape(DEV, 1, lanes), BOTH, 0, 0, tiled=True)  14.4 us
    all_to_all x1, waiting for transfers between devices, exchange(): lax.all_to_all(lines.reshape(DEV, 1, lanes), BOTH, 0, 0, tiled=True)  9.98 us
    all_to_all x1, blocking collectives, shards(): slip = lax.all_to_all(packed, 'dip', 0, 0, tiled=True)  9.81 us
    pallas_call x8, Pallas kernels, call(): pl.pallas_call(kernel, out_shape=[jax.ShapeDtypeStruct(s, F32) for s in o...  9.34 us
    all_to_all x1, blocking collectives, shards(): gathered = lax.all_to_all(out, 'dip', 0, 0, tiled=True)  8.23 us
    ppermute x3, starting transfers between devices, shards(): lax.ppermute(part, 'dip', [(j, (j + i) % 4) for j in range(4)])  5.01 us
  transfers between devices with their start and end apart: 4, of which 2 were waited for; matrix products, arithmetic and copies ran while one was open for 0% of the time, Pallas kernels for 1%

profile of v4, /device:TPU:1, one launch (start us, length us, event | category | flops | bytes accessed | tf_op | source)
XLA Modules:
  0.0 126.9 jit_solution(13117983016281065896)
XLA Ops:
  0.6 0.0 copy-start.6
  0.6 1.0 copy.12
  1.6 0.0 copy-start.7
  1.7 9.8 %all_to_all.30.fields = f32[4,48,256]{2,1,0:T(8,128)S(1)} all-to-all(f32[4,48,256]{2,1,0:T(8,128)S(1)} %bitcast.19), channel_id=1, replica_groups=mesh['strike'=64,'dip'=4] {'dip'}, dimensions={0} | all-to-all | bytes 393216 | tf_op jit(solution)/shard_map/all_to_all | solution.py:355
  11.5 1.3 %shard_map.104 = f32[768,128]{1,0:T(8,128)} custom-call(f32[4,48,256]{2,1,0:T(8,128)S(1)} %all_to_all.30.fields, f32[40,256]{1,0:T(8,128)S(1)} %copy-done.7, bf16[1280,256]{1,0:T(8,128)(2,1)S(1)} %copy-done.6), custom_call_target="tpu_custom_call" | custom-call | flops 2000000000 | bytes 6000000 | tf_op jit(solution)/shard_map/pallas_call | solution.py:334
  12.8 14.4 %all-to-all-start.1 = ((f32[256,1,384]{2,1,0:T(1,128)}), f32[256,1,384]{2,1,0:T(1,128)S(1)}, u32[]{:S(2)}, u32[]{:S(2)}) async-start(f32[256,1,384]{2,1,0:T(1,128)} %bitcast.3), calls=%async_computation.1 | async-start | bytes 786432 | tf_op jit(solution)/shard_map/all_to_all | solution.py:347
  27.3 0.0 copy-start
  27.3 0.0 copy-start.5
  27.3 1.4 %collective-permute-start = (f32[64,256]{1,0:T(8,128)S(1)}, f32[64,256]{1,0:T(8,128)S(1)}, u32[]{:S(2)}, u32[]{:S(2)}) collective-permute-start(f32[64,256]{1,0:T(8,128)S(1)} %get-tuple-element.24), channel_id=1, source_target_pairs={{0,1},{1,2},{2,3},{3,0},{4,5},{5,6},{6,7},{7,4},{8,9},{9,10},{10,1... | collective-permute-start | bytes 196616 | tf_op jit(solution)/shard_map/ppermute | solution.py:367
  28.7 2.4 %collective-permute-start.1 = (f32[64,256]{1,0:T(8,128)S(1)}, f32[64,256]{1,0:T(8,128)S(1)}, u32[]{:S(2)}, u32[]{:S(2)}) collective-permute-start(f32[64,256]{1,0:T(8,128)S(1)} %get-tuple-element.25), channel_id=1, source_target_pairs={{0,2},{1,3},{2,0},{3,1},{4,6},{5,7},{6,4},{7,5},{8,10},{9,11},{10,... | collective-permute-start | bytes 196616 | tf_op jit(solution)/shard_map/ppermute | solution.py:367
  31.1 1.2 collective-permute-start.2
  32.3 1.5 %shard_map.106 = (f32[3,128,256]{2,1,0:T(8,128)S(1)}, f32[2,128,256]{2,1,0:T(8,128)S(1)}, f32[7,64,256]{2,1,0:T(8,128)S(1)}) custom-call(bf16[4,3,2,4,4096]{4,3,2,1,0:T(4,128)(2,1)S(1)} %copy-done, s32[4,4096]{1,0:T(4,128)S(1)} %copy-done.5), custom_call_target="tpu_custom_call" | custom-call | flops 2000000000 | bytes 6000000 | tf_op jit(solution)/shard_map/pallas_call | solution.py:334
  33.8 0.0 collective-permute-done.part1
  33.9 1.8 %collective-permute-done.1.part2 = f32[64,256]{1,0:T(8,128)S(1)} collective-permute-done((f32[64,256]{1,0:T(8,128)S(1)}, f32[64,256]{1,0:T(8,128)S(1)}, u32[]{:S(2)}, u32[]{:S(2)}) %collective-permute-start.1) | collective-permute-done | bytes 65568 | tf_op jit(solution)/shard_map/ppermute | solution.py:367
  35.7 10.0 %all-to-all-done.1 = f32[256,1,384]{2,1,0:T(1,128)S(1)} async-done(((f32[256,1,384]{2,1,0:T(1,128)}), f32[256,1,384]{2,1,0:T(1,128)S(1)}, u32[]{:S(2)}, u32[]{:S(2)}) %all-to-all-start.1) | async-done | bytes 393248 | tf_op jit(solution)/shard_map/all_to_all | solution.py:347
  45.7 2.0 %shard_map.107 = (f32[768,128]{1,0:T(8,128)S(1)}, f32[2,128,256]{2,1,0:T(8,128)S(1)}) custom-call(f32[768,128]{1,0:T(8,128)S(1)} %bitcast.12, f32[3,128,256]{2,1,0:T(8,128)S(1)} %get-tuple-element.31.past, f32[2,128,256]{2,1,0:T(8,128)S(1)} %get-tuple-element.32.past_next, f32[7,64,256]{2,1,0:T(8,128)S(1)} %get-tuple-element.33.coef, ...), custom_call_target="tpu_custom_call" | custom-call | flops 2000000000 | bytes 6000000 | tf_op jit(solution)/shard_map/pallas_call | solution.py:334
  47.7 24.0 %all_to_all.31 = f32[256,1,384]{2,1,0:T(1,128)S(1)} all-to-all(f32[256,1,384]{2,1,0:T(1,128)S(1)} %bitcast.14), channel_id=1, replica_groups=mesh['strike'=64,'dip'=4] {'strike','dip'}, dimensions={0} | all-to-all | bytes 786432 | tf_op jit(solution)/shard_map/all_to_all | solution.py:347
  71.7 1.5 %shard_map.108 = (f32[512,128]{1,0:T(8,128)S(1)}, f32[64,256]{1,0:T(8,128)S(1)}, f32[3,64,256]{2,1,0:T(8,128)S(1)}, f32[64,256]{1,0:T(8,128)S(1)}) custom-call(f32[768,128]{1,0:T(8,128)S(1)} %bitcast.13, f32[64,256]{1,0:T(8,128)S(1)} %get-tuple-element.35.part0, f32[64,256]{1,0:T(8,128)S(1)} %collective-permute-done.part1, ...), custom_call_target="tpu_custom_call" | custom-call | flops 2000000000 | bytes 6000000 | tf_op jit(solution)/shard_map/pallas_call | solution.py:334
  73.2 21.3 %all_to_all.32 = f32[256,1,256]{2,1,0:T(1,128)S(1)} all-to-all(f32[256,1,256]{2,1,0:T(1,128)S(1)} %bitcast.15), channel_id=1, replica_groups=mesh['strike'=64,'dip'=4] {'strike','dip'}, dimensions={0} | all-to-all | bytes 524288 | tf_op jit(solution)/shard_map/all_to_all | solution.py:347
  94.5 1.6 %shard_map.109 = f32[512,128]{1,0:T(8,128)S(1)} custom-call(f32[512,128]{1,0:T(8,128)S(1)} %bitcast.17, f32[2,128,256]{2,1,0:T(8,128)S(1)} %get-tuple-element.40.older, f32[7,64,256]{2,1,0:T(8,128)S(1)} %get-tuple-element.33.coef, f32[40,256]{1,0:T(8,128)S(1)} %copy-done.7, bf16[1280,256]{1,0:T(8,128)(2,1)S(1)} %copy-done.6), custom_call_target="tpu_custom_call" | custom-call | flops 2000000000 | bytes 6000000 | tf_op jit(solution)/shard_map/pallas_call | solution.py:334
  96.1 21.2 %all_to_all.33 = f32[256,1,256]{2,1,0:T(1,128)S(1)} all-to-all(f32[256,1,256]{2,1,0:T(1,128)S(1)} %bitcast.18), channel_id=1, replica_groups=mesh['strike'=64,'dip'=4] {'strike','dip'}, dimensions={0} | all-to-all | bytes 524288 | tf_op jit(solution)/shard_map/all_to_all | solution.py:347
  117.3 0.6 shard_map.110
  118.0 8.2 %all_to_all.34.gathered = f32[4,64,256]{2,1,0:T(8,128)S(1)} all-to-all(f32[4,64,256]{2,1,0:T(8,128)S(1)} %shard_map.110), channel_id=1, replica_groups=mesh['strike'=64,'dip'=4] {'dip'}, dimensions={0} | all-to-all | bytes 524288 | tf_op jit(solution)/shard_map/all_to_all | solution.py:395
  126.2 0.7 shard_map.111
  (14 shorter events, 0.1 us)
Async XLA Ops:
  0.6 10.8 %copy-start.6 = (bf16[1280,256]{1,0:T(8,128)(2,1)S(1)}, bf16[1280,256]{1,0:T(8,128)(2,1)}, u32[]{:S(2)}) copy-start(bf16[1280,256]{1,0:T(8,128)(2,1)} %constant.5.clone.mats) | copy-start | bytes 1966084
  1.6 9.8 %copy-start.7 = (f32[40,256]{1,0:T(8,128)S(1)}, f32[40,256]{1,0:T(8,128)}, u32[]{:S(2)}) copy-start(f32[40,256]{1,0:T(8,128)} %constant.4.clone.angles) | copy-start | bytes 122884
  12.8 14.4 %copy-start.1 = (f32[2,64,256]{2,1,0:T(8,128)S(1)}, f32[2,64,256]{2,1,0:T(8,128)}, u32[]{:S(2)}) copy-start(f32[2,64,256]{2,1,0:T(8,128)} %prestress.1) | copy-start | bytes 393220
  12.8 14.4 %copy-start.2 = (f32[64,256]{1,0:T(8,128)S(1)}, f32[64,256]{1,0:T(8,128)}, u32[]{:S(2)}) copy-start(f32[64,256]{1,0:T(8,128)} %normal.1) | copy-start | bytes 196612
  12.8 14.4 %copy-start.3 = (f32[64,256]{1,0:T(8,128)S(1)}, f32[64,256]{1,0:T(8,128)}, u32[]{:S(2)}) copy-start(f32[64,256]{1,0:T(8,128)} %effect.1) | copy-start | bytes 196612
  12.8 14.5 %copy-start.4 = (f32[64,256]{1,0:T(8,128)S(1)}, f32[64,256]{1,0:T(8,128)}, u32[]{:S(2)}) copy-start(f32[64,256]{1,0:T(8,128)} %state.1) | copy-start | bytes 196612
  12.8 32.9 %all-to-all-start.1 = ((f32[256,1,384]{2,1,0:T(1,128)}), f32[256,1,384]{2,1,0:T(1,128)S(1)}, u32[]{:S(2)}, u32[]{:S(2)}) async-start(f32[256,1,384]{2,1,0:T(1,128)} %bitcast.3), calls=%async_computation.1 | async-start | bytes 786432 | tf_op jit(solution)/shard_map/all_to_all | solution.py:347
  27.3 5.1 %copy-start = (bf16[4,3,2,4,4096]{4,3,2,1,0:T(4,128)(2,1)S(1)}, bf16[4,3,2,4,4096]{4,3,2,1,0:T(4,128)(2,1)}, u32[]{:S(2)}) copy-start(bf16[4,3,2,4,4096]{4,3,2,1,0:T(4,128)(2,1)} %history.1) | copy-start | bytes 2359300
  27.3 5.1 %copy-start.5 = (s32[4,4096]{1,0:T(4,128)S(1)}, s32[4,4096]{1,0:T(4,128)}, u32[]{:S(2)}) copy-start(s32[4,4096]{1,0:T(4,128)} %lengths.1) | copy-start | bytes 196612
  27.3 6.5 %collective-permute-start = (f32[64,256]{1,0:T(8,128)S(1)}, f32[64,256]{1,0:T(8,128)S(1)}, u32[]{:S(2)}, u32[]{:S(2)}) collective-permute-start(f32[64,256]{1,0:T(8,128)S(1)} %get-tuple-element.24), channel_id=1, source_target_pairs={{0,1},{1,2},{2,3},{3,0},{4,5},{5,6},{6,7},{7,4},{8,9},{9,10},{10,1... | collective-permute-start | bytes 196616 | tf_op jit(solution)/shard_map/ppermute | solution.py:367
  28.7 6.9 %collective-permute-start.1 = (f32[64,256]{1,0:T(8,128)S(1)}, f32[64,256]{1,0:T(8,128)S(1)}, u32[]{:S(2)}, u32[]{:S(2)}) collective-permute-start(f32[64,256]{1,0:T(8,128)S(1)} %get-tuple-element.25), channel_id=1, source_target_pairs={{0,2},{1,3},{2,0},{3,1},{4,6},{5,7},{6,4},{7,5},{8,10},{9,11},{10,... | collective-permute-start | bytes 196616 | tf_op jit(solution)/shard_map/ppermute | solution.py:367
  31.1 4.5 %collective-permute-start.2 = (f32[64,256]{1,0:T(8,128)S(1)}, f32[64,256]{1,0:T(8,128)S(1)}, u32[]{:S(2)}, u32[]{:S(2)}) collective-permute-start(f32[64,256]{1,0:T(8,128)S(1)} %get-tuple-element.26), channel_id=1, source_target_pairs={{0,3},{1,0},{2,1},{3,2},{4,7},{5,4},{6,5},{7,6},{8,11},{9,8},{10,9... | collective-permute-start | bytes 196616 | tf_op jit(solution)/shard_map/ppermute | solution.py:367

commit v5 on v4

--- a/solution.py
+++ b/solution.py
@@ -64,10 +64,23 @@
     return table.reshape(2 * MODES, DEV).astype(np.float32)
 
 
+def flip_tables():
+    lanes = np.zeros((DEV, DEV))
+    lanes[np.arange(DEV), -np.arange(DEV) % DEV] = 1.0
+    rows = np.zeros((2, ROWS, MODES, DEV))
+    for k1 in range(ROWS):
+        for m in range(MODES):
+            rows[0, k1, m, (15 - k1) * MODES + m] = 1.0
+            rows[1, k1, m, (-k1 % ROWS) * MODES + m] = 1.0
+    table = np.concatenate([lanes, rows.reshape(128, DEV)], 0)
+    return table.astype(np.float32).astype(jnp.bfloat16)
+
+
 def matrix_tables():
     dft = dft_table().reshape(4 * DEV, DEV)
     sides = [split_table(t) for t in (inner_table(-1.0), inverse_inner())]
-    return np.concatenate([dft] + [np.concatenate([t[0], t[1]], 1) for t in sides], 0)
+    sides = [np.concatenate([t[0], t[1]], 1) for t in sides]
+    return np.concatenate([dft] + sides + [flip_tables()], 0)
 
 
 def angle_tables():
@@ -113,6 +126,59 @@
         ref[pl.ds(c, DEV, stride=len(blocks)), :] = jnp.concatenate([real, imag], 0).T
 
 
+def position():
+    return lax.axis_index("strike") * 4 + lax.axis_index("dip")
+
+
+def send_half(ref, field, angles, mats):
+    halves = ([], [])
+    lasts = []
+    lane = lax.broadcasted_iota(jnp.int32, (16, DEV), 1)
+    sign = 1.0 - 2.0 * (lane & 1).astype(F32)
+    for real, imag in dip_forward(field, angles):
+        lasts.append(jnp.sum(real[:16] * sign, 1, keepdims=True))
+        for rows, at in zip(halves, (0, 16)):
+            re, im = real[at : at + 32], imag[at : at + 32]
+            rows.append(jnp.concatenate([re, im], 1))
+            rows.append(jnp.concatenate([im, -re], 1))
+    outs = []
+    for rows, lanes in zip(halves, (slice(0, 128), slice(128, 256))):
+        table = (mats[: 2 * DEV, lanes], mats[2 * DEV : 4 * DEV, lanes])
+        outs.append(dot3(split(jnp.concatenate(rows, 0)), table))
+    out = jnp.concatenate(outs, 1)
+    pieces = []
+    for c, last in enumerate(lasts):
+        pieces.append(out[64 * c : 64 * c + 32])
+        pieces.append(jnp.where(lane == 0, last, out[64 * c + 32 : 64 * c + 48]))
+        pieces.append(out[64 * c + 48 : 64 * c + 64])
+    if len(lasts) == 2:
+        ref[...] = jnp.concatenate(pieces, 0).T
+    else:
+        ref[pl.ds(0, DEV, stride=2), :] = jnp.concatenate(pieces[:6], 0).T
+        pieces.append(jnp.zeros((64, DEV), F32))
+        ref[pl.ds(1, DEV, stride=2), :] = jnp.concatenate(pieces[6:], 0).T
+
+
+def receive_half(ref, count):
+    device = position()
+    low = jnp.where(device < DEV // 2, 1.0, 0.0)
+    zero = jnp.where(device == 0, 1.0, 0.0)
+    up = 1.0 - low
+    if count == 2:
+        lines = [ref[...].T]
+    else:
+        lines = [ref[pl.ds(i, DEV, stride=2), :].T for i in range(2)]
+    blocks = []
+    for c in range(count):
+        line = lines[c // 2][64 * (c % 2) : 64 * (c % 2) + 64]
+        ar, br, ai, bi = [line[16 * i : 16 * i + 16] for i in range(4)]
+        none = jnp.zeros_like(ar)
+        real = [low * ar, low * br + up * ar, up * br + zero * ai, none]
+        imag = [(low - zero) * ai, low * bi + up * ai, up * bi, none]
+        blocks.append((jnp.concatenate(real, 0), jnp.concatenate(imag, 0)))
+    return blocks
+
+
 def turns(angles):
     cos = [angles[32 + m : 33 + m, :] for m in range(4)]
     sin = [angles[36 + m : 37 + m, :] for m in range(4)]
@@ -136,16 +202,21 @@
     return blocks
 
 
-def dip_inverse(blocks, angles):
+def dip_inverse(lines, angles, mats):
+    lasts = [imag[:16, :1] for _, imag in lines]
+    blocks = long_dft(lines, mats, 1)
     cos, sin = turns(angles)
+    lane = lax.broadcasted_iota(jnp.int32, (16, DEV), 1)
+    sign = (1.0 - 2.0 * (lane & 1).astype(F32)) * (1.0 / math.sqrt(NZ))
     field = []
-    for real, imag in blocks:
+    for (real, imag), last in zip(blocks, lasts):
         re = [real[16 * m : 16 * m + 16] for m in range(4)]
         im = [imag[16 * m : 16 * m + 16] for m in range(4)]
         u = [cos[m] * re[m] - sin[m] * im[m] for m in range(4)]
         v1 = cos[1] * im[1] + sin[1] * re[1]
         v3 = cos[3] * im[3] + sin[3] * re[3]
         a, b, c, d = u[0] + u[2], u[0] - u[2], u[1] + u[3], v3 - v1
+        a, b = a + sign * last, b + sign * last
         field.append(jnp.concatenate([a + c, b + d, a - c, b - d], 0))
     return field
 
@@ -180,7 +251,7 @@
 
 def first_kernel(fields, angles, mats, out):
     field = [[fields[d, 16 * c : 16 * c + 16, :] for d in range(4)] for c in range(3)]
-    write_lines(out, long_dft(dip_forward(field, angles), mats, -1))
+    send_half(out, field, angles, mats)
 
 
 def middle_kernel(lines, part0, part1, part2, part3, angles, mats, out, state_out, fields, opening):
@@ -190,16 +261,16 @@
         for c in range(3):
             fields[c, rows, :] = part[16 * c : 16 * c + 16, :]
         state_out[rows, :] = part[48:64, :]
-    force = dip_inverse(long_dft(read_lines(lines, (0, 1, 2), 3), mats, 1), angles)
+    force = dip_inverse(read_lines(lines, (0, 1, 2), 3), angles, mats)
     opening[...] = 2.0 * force[2]
     rates, state = friction(force, (fields[0], fields[1]), fields[2], state_out[...])
     state_out[...] = state
     field = [[r[16 * d : 16 * d + 16] for d in range(4)] for r in rates]
-    write_lines(out, long_dft(dip_forward(field, angles), mats, -1))
+    send_half(out, field, angles, mats)
 
 
 def last_kernel(lines, fields, state_in, opening, angles, mats, out):
-    force = dip_inverse(long_dft(read_lines(lines, (0, 1), 2), mats, 1), angles)
+    force = dip_inverse(read_lines(lines, (0, 1), 2), angles, mats)
     rates, state = friction(force, (fields[0], fields[1]), fields[2], state_in[...])
     for d in range(4):
         for c, value in enumerate(rates + [opening, state]):
@@ -214,11 +285,8 @@
         state[rows, :] = gathered[d, 48:64, :]
 
 
-def mixing(device):
-    shape = (64, DEV)
-    row = lax.broadcasted_iota(jnp.int32, shape, 0)
-    kx = (row >> 2) * DEV + lax.broadcasted_iota(jnp.int32, shape, 1)
-    kz = device * MODES + (row & 3)
+def mixing(kz, kx, lags):
+    shape = kz.shape
     mz = jnp.where(2 * kz < NZ, kz, kz - NZ)
     mx = jnp.where(2 * kx < NX, kx, kx - NX)
     qz = mz.astype(F32) * (2.0 * math.pi / NZ)
@@ -235,7 +303,7 @@
     before = [jnp.ones(shape, F32)] * 3
     now = first
     out = []
-    for lag in range(4):
+    for _ in range(lags):
         envelope = envelope * decay
         two, three, one = [envelope * c for c in now]
         out.append((xx * two + zz * three, xz * (two - three), zz * two + xx * three, one))
@@ -243,44 +311,98 @@
     return out
 
 
-def history_kernel(history, lengths, past1, past2, coef, held, reach):
-    device = lax.axis_index("strike") * 4 + lax.axis_index("dip")
-    for k1 in range(16):
-        lanes = slice(DEV * k1, DEV * k1 + DEV)
-        rows = slice(4 * k1, 4 * k1 + 4)
-        reach[rows, :] = lengths[:, lanes].astype(F32)
+def spread(lengths):
+    line = lengths[...].astype(F32)
+    return jnp.concatenate([line[:, DEV * k1 : DEV * k1 + DEV] for k1 in range(16)], 0)
+
+
+def flip(arrays, mats):
+    lanes, rows = mats[1280:1536, :], (mats[1536:1600, :64], mats[1600:1664, :64])
+    first = lax.broadcasted_iota(jnp.int32, (64, DEV), 1) == 0
+    turned = sum(
+        jnp.dot(part, lanes, preferred_element_type=F32)
+        for part in split(jnp.concatenate(arrays, 0))
+    )
+    count = len(arrays)
+    parts = split(jnp.concatenate([turned[64 * i : 64 * i + 64] for i in range(count)], 1))
+    wide = [sum(jnp.dot(r, p, preferred_element_type=F32) for p in parts) for r in rows]
+    return [
+        jnp.where(first, *[w[:, DEV * i : DEV * i + DEV] for w in (wide[1], wide[0])])
+        for i in range(count)
+    ]
+
+
+def history_kernel(history, lengths, across, beside, mats, past1, past2, coef, held):
+    device = position()
     for lag in range(3):
         for c in range(3):
             for part in range(2):
                 line = history[lag, c, part].astype(F32)
                 for k1 in range(16):
                     held[lag, c, part, 4 * k1 : 4 * k1 + 4, :] = line[:, DEV * k1 : DEV * k1 + DEV]
-    mix = mixing(device)
-    length = reach[...]
+    shape = (64, DEV)
+    row = lax.broadcasted_iota(jnp.int32, shape, 0)
+    kx = (row >> 2) * DEV + lax.broadcasted_iota(jnp.int32, shape, 1)
+    m = row & 3
+    zero = device == 0
+    upper = jnp.where(device < DEV // 2, 0, 1)
+    origin = jnp.where(zero, 0, 64)
+    anchor = (m + origin) == 0
+    guest = (m + origin) == 2
+    length = spread(lengths)
+    mix = mixing(device * MODES + m, kx, 4)
     masked = [None] + [
-        [jnp.where(length > float(lag), m, 0.0) for m in mix[lag]] for lag in range(1, 4)
+        [jnp.where(length > float(lag), v, 0.0) for v in mix[lag]] for lag in range(1, 4)
     ]
-    twice = 2.0 * mix[0][3]
-    for i in range(3):
-        coef[i] = mix[0][i]
-        coef[4 + i] = masked[1][i]
-    coef[3] = twice * mix[0][3] + masked[1][3]
+
+    def active(value):
+        return jnp.where(value > 1.0, 1.0, 0.0)
+
+    other = active(spread(beside))
+    own = active(length)
+    own_back, across_back, other_back = flip([own, active(spread(across)), other], mats)
+    own = jnp.where(guest, pltpu.roll(other, 2, 0), own)
+    back = jnp.where(m == 1, pltpu.roll(across_back, 62, 0), across_back)
+    back = jnp.where(m == 0, other_back, back)
+    back = jnp.where(anchor, own_back, back)
+    back = jnp.where(guest, pltpu.roll(other_back, 2, 0), back)
+    mine = (m == upper) | (m == upper + 1)
+    weight = jnp.where(mine, 1.0, 0.0)
+    weight = jnp.where(anchor | guest, 0.5, weight)
+    nyquist = kx == NX // 2
+    total, cross = own + back, jnp.where(nyquist, own - back, own + back)
+    cross = jnp.where(guest, jnp.where(nyquist, total, own - back), cross)
+    cross0 = jnp.where(nyquist, 0.0, 2.0 * weight)
+    cross0 = jnp.where(guest, jnp.where(nyquist, 1.0, 0.0), cross0)
+    new, old = mixing(jnp.where(guest, NZ // 2, device * MODES + m), kx, 2)
+    coef[0] = 2.0 * weight * new[0]
+    coef[1] = cross0 * new[1]
+    coef[2] = 2.0 * weight * new[2]
+    coef[3] = weight * (4.0 * new[3] * new[3] + total * old[3])
+    coef[4] = weight * total * old[0]
+    coef[5] = weight * cross * old[1]
+    coef[6] = weight * total * old[2]
+    coef[7] = jnp.where(guest, 1.0, 0.0)
+    sums = []
     for part in range(2):
-        rows = slice(64 * part, 64 * part + 64)
         totals = []
         for skip in (1, 2):
-            total = [0.0, 0.0, 0.0]
+            value = [0.0, 0.0, 0.0]
             for lag in range(skip, 4):
                 ss, sd, dd, op = masked[lag]
                 a, b, c = [held[lag - skip, i, part] for i in range(3)]
-                total[0] = total[0] + (ss * a + sd * b)
-                total[1] = total[1] + (sd * a + dd * b)
-                total[2] = total[2] + op * c
-            totals.append(total)
-        for i in range(2):
-            past1[i, rows, :] = totals[0][i]
-            past2[i, rows, :] = totals[1][i]
-        past1[2, rows, :] = twice * totals[0][2] + totals[1][2]
+                value[0] = value[0] + (ss * a + sd * b)
+                value[1] = value[1] + (sd * a + dd * b)
+                value[2] = value[2] + op * c
+            totals.append(value)
+        one, two = totals
+        sums.append([one[0], one[1], 2.0 * mix[0][3] * one[2] + two[2], two[0], two[1]])
+    turned = flip(sums[0] + sums[1], mats)
+    for i in range(5):
+        target = past1.at[i] if i < 3 else past2.at[i - 3]
+        re, im = sums[0][i], sums[1][i]
+        target[0:64, :] = jnp.where(anchor, 0.5 * (re + turned[i]), re)
+        target[64:128, :] = jnp.where(anchor, 0.5 * (im - turned[5 + i]), im)
 
 
 def spectrum_of(blocks, angles, mats):
@@ -306,26 +428,33 @@
     write_lines(out, long_dft(turned, mats, 1))
 
 
-def both_parts(coef, i):
-    return jnp.concatenate([coef[i]] * 2, 0)
+def settle(coef, real, imag):
+    guest = coef[7]
+    gr, gi = guest * real, guest * imag
+    real, imag = real - gr - pltpu.roll(gi, 62, 0), imag - gi + pltpu.roll(gr, 62, 0)
+    return jnp.concatenate([real, imag], 0)
 
 
 def apply_mix(coef, at, spec):
-    ss, sd, dd = [both_parts(coef, at + i) for i in range(3)]
-    s, d = spec[:, :DEV], spec[:, DEV : 2 * DEV]
-    return [ss * s + sd * d, sd * s + dd * d]
+    out = [[], []]
+    for rows in (slice(0, 64), slice(64, 128)):
+        s, d = spec[rows, :DEV], spec[rows, DEV : 2 * DEV]
+        out[0].append(coef[at] * s + coef[at + 1] * d)
+        out[1].append(coef[at + 1] * s + coef[at + 2] * d)
+    return [settle(coef, *parts) for parts in out]
 
 
 def mode_kernel_first(lines, past, past_next, coef, angles, mats, out, older):
-    spec = spectrum_of(read_lines(lines, (0, 1, 2), 3), angles, mats)
+    spec = spectrum_of(receive_half(lines, 3), angles, mats)
     for c, f in enumerate(apply_mix(coef, 4, spec)):
         older[c] = f + past_next[c]
-    force = apply_mix(coef, 0, spec) + [both_parts(coef, 3) * spec[:, 2 * DEV :]]
+    opening = [coef[3] * spec[rows, 2 * DEV :] for rows in (slice(0, 64), slice(64, 128))]
+    force = apply_mix(coef, 0, spec) + [settle(coef, *opening)]
     lines_of(out, [f + past[c] for c, f in enumerate(force)], angles, mats)
 
 
 def mode_kernel_second(lines, older, coef, angles, mats, out):
-    spec = spectrum_of(read_lines(lines, (0, 1), 2), angles, mats)
+    spec = spectrum_of(receive_half(lines, 2), angles, mats)
     force = apply_mix(coef, 0, spec)
     lines_of(out, [f + older[c] for c, f in enumerate(force)], angles, mats)
 
@@ -350,10 +479,13 @@
 
 def shards(slip_rate, history, lengths, prestress, normal_stress, direct_effect, state_log):
     mats, angles = matrix_tables(), angle_tables()
-    three, two = (3 * DEV, 128), (2 * DEV, 128)
+    three, two, one = (3 * DEV, 128), (2 * DEV, 128), (DEV, 128)
+    across = lax.ppermute(lengths, BOTH, [(j, DEV - 1 - j) for j in range(DEV)])
+    beside = [(DEV - j, j) for j in range(1, DEV // 2)] + [(DEV // 2, 0)]
+    beside = lax.ppermute(lengths, BOTH, beside)
     packed = slip_rate.reshape(3, 4, 16, 256).transpose(1, 0, 2, 3).reshape(4, 48, 256)
     slip = lax.all_to_all(packed, "dip", 0, 0, tiled=True)
-    (out,) = call(first_kernel, [three], slip, angles, mats)
+    (out,) = call(first_kernel, [two], slip, angles, mats)
     lines = exchange(out)
     parts = call(
         pack_rest_kernel,
@@ -369,10 +501,13 @@
     ]
     past1, past2, coef = call(
         history_kernel,
-        [(3, 128, 256), (2, 128, 256), (7, 64, 256)],
+        [(3, 128, 256), (2, 128, 256), (8, 64, 256)],
         history,
         lengths,
-        scratch=[pltpu.VMEM((3, 3, 2, 64, 256), F32), pltpu.VMEM((64, 256), F32)],
+        across,
+        beside,
+        mats,
+        scratch=[pltpu.VMEM((3, 3, 2, 64, 256), F32)],
     )
     lines, parts, past1, past2, coef = lax.optimization_barrier(
         (lines, parts, past1, past2, coef)
@@ -382,7 +517,7 @@
     )
     out, state, fields, opening = call(
         middle_kernel,
-        [two, (64, 256), (3, 64, 256), (64, 256)],
+        [one, (64, 256), (3, 64, 256), (64, 256)],
         exchange(out),
         *parts,
         angles,

time: 127 us -> 133 us (1.047)
  starting transfers between devices: 19.4 us -> 27.6 us
  waiting for transfers between devices: 11.8 us -> 4.63 us
  blocking collectives: 84.6 us -> 86.4 us
  Pallas kernels: 9.34 us -> 11 us
    ppermute x0 -> x2, starting transfers between devices: none -> 10.4 us  [the longest x1 9.14 us: shards(): across = lax.ppermute(lengths, BOTH, [(j, DEV - 1 - j) for j in range(DEV)])]
    all_to_all x1, waiting for transfers between devices: 9.98 us -> 0.01 us  [exchange(): lax.all_to_all(lines.reshape(DEV, 1, lanes), BOTH, 0, 0, tiled=True)]
    ppermute x0 -> x2, waiting for transfers between devices: none -> 4.62 us  [the longest x1 3.9 us: shards(): across = lax.ppermute(lengths, BOTH, [(j, DEV - 1 - j) for j in range(DEV)])]
    ppermute x3, starting transfers between devices: 5.01 us -> 2.75 us  [shards(): lax.ppermute(part, 'dip', [(j, (j + i) % 4) for j in range(4)])]
    all_to_all x3, blocking collectives: 66.5 us -> 68.4 us  [exchange(): lax.all_to_all(lines.reshape(DEV, 1, lanes), BOTH, 0, 0, tiled=True)]
    ppermute x3, waiting for transfers between devices: 1.83 us -> 0.01 us  [shards(): lax.ppermute(part, 'dip', [(j, (j + i) % 4) for j in range(4)])]
    pallas_call x8, Pallas kernels: 9.34 us -> 11 us  [call(): pl.pallas_call(kernel, out_shape=[jax.ShapeDtypeStruct(s, F32) for s in o...]
  transfers between devices with their start and end apart: 4 -> 6, of which waited for: 2 -> 2; matrix products, arithmetic and copies ran while one was open for 0% -> 0% of each run, Pallas kernels for 1% -> 2%
where the time goes in v5:
time: 133 us
  blocking collectives  86.4 us (65%)
  starting transfers between devices  27.6 us (21%)
  Pallas kernels  11 us (8%)
  waiting for transfers between devices  4.63 us (3%)
  local copies, waits for them, and re-layouts  2.14 us (2%)
    all_to_all x3, blocking collectives, exchange(): lax.all_to_all(lines.reshape(DEV, 1, lanes), BOTH, 0, 0, tiled=True)  68.4 us
    all_to_all x1, starting transfers between devices, exchange(): lax.all_to_all(lines.reshape(DEV, 1, lanes), BOTH, 0, 0, tiled=True)  14.4 us
    pallas_call x8, Pallas kernels, call(): pl.pallas_call(kernel, out_shape=[jax.ShapeDtypeStruct(s, F32) for s in o...  11 us
    all_to_all x1, blocking collectives, shards(): slip = lax.all_to_all(packed, 'dip', 0, 0, tiled=True)  9.81 us
    ppermute x1, starting transfers between devices, shards(): across = lax.ppermute(lengths, BOTH, [(j, DEV - 1 - j) for j in range(DEV)])  9.14 us
    all_to_all x1, blocking collectives, shards(): gathered = lax.all_to_all(out, 'dip', 0, 0, tiled=True)  8.23 us
    ppermute x1, waiting for transfers between devices, shards(): across = lax.ppermute(lengths, BOTH, [(j, DEV - 1 - j) for j in range(DEV)])  3.9 us
    ppermute x3, starting transfers between devices, shards(): lax.ppermute(part, 'dip', [(j, (j + i) % 4) for j in range(4)])  2.75 us
  transfers between devices with their start and end apart: 6, of which 2 were waited for; matrix products, arithmetic and copies ran while one was open for 0% of the time, Pallas kernels for 2%

profile of v5, /device:TPU:1, one launch (start us, length us, event | category | flops | bytes accessed | tf_op | source)
XLA Modules:
  0.0 132.6 jit_solution(738490514366913880)
XLA Ops:
  0.6 0.9 copy.12
  1.6 0.0 copy-start.8
  1.6 9.8 %all_to_all.30.fields = f32[4,48,256]{2,1,0:T(8,128)S(1)} all-to-all(f32[4,48,256]{2,1,0:T(8,128)S(1)} %bitcast.21), channel_id=1, replica_groups=mesh['strike'=64,'dip'=4] {'dip'}, dimensions={0} | all-to-all | bytes 393216 | tf_op jit(solution)/shard_map/all_to_all | solution.py:487
  11.4 1.2 copy-done.6
  12.6 1.2 shard_map.104
  13.8 14.4 %all-to-all-start.1 = ((f32[256,1,256]{2,1,0:T(1,128)}), f32[256,1,256]{2,1,0:T(1,128)S(1)}, u32[]{:S(2)}, u32[]{:S(2)}) async-start(f32[256,1,256]{2,1,0:T(1,128)} %bitcast.3), calls=%async_computation.1 | async-start | bytes 524288 | tf_op jit(solution)/shard_map/all_to_all | solution.py:476
  28.3 0.0 copy-start.7
  28.3 9.1 %collective-permute-start.3 = (s32[4,4096]{1,0:T(4,128)S(1)}, s32[4,4096]{1,0:T(4,128)S(1)}, u32[]{:S(2)}, u32[]{:S(2)}) collective-permute-start(s32[4,4096]{1,0:T(4,128)S(1)} %copy-done.5), channel_id=1, source_target_pairs={{0,255},{1,254},{2,253},{3,252},{4,251},{5,250},{6,249},{7,248},{8... | collective-permute-start | bytes 196616 | tf_op jit(solution)/shard_map/ppermute | solution.py:483
  37.4 1.3 collective-permute-start.4
  38.8 0.1 collective-permute-start
  38.9 1.4 %collective-permute-start.1 = (f32[64,256]{1,0:T(8,128)S(1)}, f32[64,256]{1,0:T(8,128)S(1)}, u32[]{:S(2)}, u32[]{:S(2)}) collective-permute-start(f32[64,256]{1,0:T(8,128)S(1)} %get-tuple-element.25), channel_id=1, source_target_pairs={{0,2},{1,3},{2,0},{3,1},{4,6},{5,7},{6,4},{7,5},{8,10},{9,11},{10,... | collective-permute-start | bytes 196616 | tf_op jit(solution)/shard_map/ppermute | solution.py:499
  40.3 1.3 collective-permute-start.2
  41.5 3.9 %collective-permute-done.3.across = s32[4,4096]{1,0:T(4,128)S(1)} collective-permute-done((s32[4,4096]{1,0:T(4,128)S(1)}, s32[4,4096]{1,0:T(4,128)S(1)}, u32[]{:S(2)}, u32[]{:S(2)}) %collective-permute-start.3) | collective-permute-done | bytes 65568 | tf_op jit(solution)/shard_map/ppermute | solution.py:483
  45.4 0.7 collective-permute-done.4.beside
  46.2 3.0 %shard_map.106 = (f32[3,128,256]{2,1,0:T(8,128)S(1)}, f32[2,128,256]{2,1,0:T(8,128)S(1)}, f32[8,64,256]{2,1,0:T(8,128)S(1)}) custom-call(bf16[4,3,2,4,4096]{4,3,2,1,0:T(4,128)(2,1)S(1)} %copy-done, s32[4,4096]{1,0:T(4,128)S(1)} %copy-done.5, s32[4,4096]{1,0:T(4,128)S(1)} %collective-permute-done.3.across, s32[4,4096]{1,0:T(4,128)S(1)} %collective-permute-done.4.beside, ...), custom_call_target="tpu_custom_call" | custom-call | flops 2000000000 | bytes 6000000 | tf_op jit(solution)/shard_map/pallas_call | solution.py:463
  49.3 2.2 %shard_map.107 = (f32[768,128]{1,0:T(8,128)S(1)}, f32[2,128,256]{2,1,0:T(8,128)S(1)}) custom-call(f32[512,128]{1,0:T(8,128)S(1)} %bitcast.16, f32[3,128,256]{2,1,0:T(8,128)S(1)} %get-tuple-element.31.past, f32[2,128,256]{2,1,0:T(8,128)S(1)} %get-tuple-element.32.past_next, f32[8,64,256]{2,1,0:T(8,128)S(1)} %get-tuple-element.33.coef, ...), custom_call_target="tpu_custom_call" | custom-call | flops 2000000000 | bytes 6000000 | tf_op jit(solution)/shard_map/pallas_call | solution.py:463
  51.4 28.3 %all_to_all.31 = f32[256,1,384]{2,1,0:T(1,128)S(1)} all-to-all(f32[256,1,384]{2,1,0:T(1,128)S(1)} %bitcast.15), channel_id=1, replica_groups=mesh['strike'=64,'dip'=4] {'strike','dip'}, dimensions={0} | all-to-all | bytes 786432 | tf_op jit(solution)/shard_map/all_to_all | solution.py:476
  79.7 1.5 %shard_map.108 = (f32[256,128]{1,0:T(8,128)S(1)}, f32[64,256]{1,0:T(8,128)S(1)}, f32[3,64,256]{2,1,0:T(8,128)S(1)}, f32[64,256]{1,0:T(8,128)S(1)}) custom-call(f32[768,128]{1,0:T(8,128)S(1)} %bitcast.14, f32[64,256]{1,0:T(8,128)S(1)} %get-tuple-element.35.part0, f32[64,256]{1,0:T(8,128)S(1)} %collective-permute-done.part1, ...), custom_call_target="tpu_custom_call" | custom-call | flops 2000000000 | bytes 6000000 | tf_op jit(solution)/shard_map/pallas_call | solution.py:463
  81.3 18.5 %all_to_all.32 = f32[256,1,128]{2,1,0:T(1,128)S(1)} all-to-all(f32[256,1,128]{2,1,0:T(1,128)S(1)} %bitcast.19), channel_id=1, replica_groups=mesh['strike'=64,'dip'=4] {'strike','dip'}, dimensions={0} | all-to-all | bytes 262144 | tf_op jit(solution)/shard_map/all_to_all | solution.py:476
  99.7 1.7 %shard_map.109 = f32[512,128]{1,0:T(8,128)S(1)} custom-call(f32[256,128]{1,0:T(8,128)S(1)} %bitcast.20, f32[2,128,256]{2,1,0:T(8,128)S(1)} %get-tuple-element.40.older, f32[8,64,256]{2,1,0:T(8,128)S(1)} %get-tuple-element.33.coef, f32[40,256]{1,0:T(8,128)S(1)} %copy-done.8, bf16[1664,256]{1,0:T(8,128)(2,1)S(1)} %copy-done.7), custom_call_target="tpu_custom_call" | custom-call | flops 2000000000 | bytes 6000000 | tf_op jit(solution)/shard_map/pallas_call | solution.py:463
  101.4 21.6 %all_to_all.33 = f32[256,1,256]{2,1,0:T(1,128)S(1)} all-to-all(f32[256,1,256]{2,1,0:T(1,128)S(1)} %bitcast.18), channel_id=1, replica_groups=mesh['strike'=64,'dip'=4] {'strike','dip'}, dimensions={0} | all-to-all | bytes 524288 | tf_op jit(solution)/shard_map/all_to_all | solution.py:476
  123.0 0.6 shard_map.110
  123.6 8.2 %all_to_all.34.gathered = f32[4,64,256]{2,1,0:T(8,128)S(1)} all-to-all(f32[4,64,256]{2,1,0:T(8,128)S(1)} %shard_map.110), channel_id=1, replica_groups=mesh['strike'=64,'dip'=4] {'dip'}, dimensions={0} | all-to-all | bytes 524288 | tf_op jit(solution)/shard_map/all_to_all | solution.py:530
  131.9 0.7 shard_map.111
  (20 shorter events, 0.1 us)
Async XLA Ops:
  1.6 9.8 %copy-start.8 = (f32[40,256]{1,0:T(8,128)S(1)}, f32[40,256]{1,0:T(8,128)}, u32[]{:S(2)}) copy-start(f32[40,256]{1,0:T(8,128)} %constant.4.clone.angles) | copy-start | bytes 122884
  11.4 1.2 copy-start.6
  13.8 14.4 %copy-start.5 = (s32[4,4096]{1,0:T(4,128)S(1)}, s32[4,4096]{1,0:T(4,128)}, u32[]{:S(2)}) copy-start(s32[4,4096]{1,0:T(4,128)} %lengths.1) | copy-start | bytes 196612
  13.8 24.9 %copy-start.1 = (f32[2,64,256]{2,1,0:T(8,128)S(1)}, f32[2,64,256]{2,1,0:T(8,128)}, u32[]{:S(2)}) copy-start(f32[2,64,256]{2,1,0:T(8,128)} %prestress.1) | copy-start | bytes 393220
  13.8 24.9 %copy-start.2 = (f32[64,256]{1,0:T(8,128)S(1)}, f32[64,256]{1,0:T(8,128)}, u32[]{:S(2)}) copy-start(f32[64,256]{1,0:T(8,128)} %normal.1) | copy-start | bytes 196612
  13.8 24.9 %copy-start.3 = (f32[64,256]{1,0:T(8,128)S(1)}, f32[64,256]{1,0:T(8,128)}, u32[]{:S(2)}) copy-start(f32[64,256]{1,0:T(8,128)} %effect.1) | copy-start | bytes 196612
  13.8 24.9 %copy-start.4 = (f32[64,256]{1,0:T(8,128)S(1)}, f32[64,256]{1,0:T(8,128)}, u32[]{:S(2)}) copy-start(f32[64,256]{1,0:T(8,128)} %state.1) | copy-start | bytes 196612
  13.8 35.4 %all-to-all-start.1 = ((f32[256,1,256]{2,1,0:T(1,128)}), f32[256,1,256]{2,1,0:T(1,128)S(1)}, u32[]{:S(2)}, u32[]{:S(2)}) async-start(f32[256,1,256]{2,1,0:T(1,128)} %bitcast.3), calls=%async_computation.1 | async-start | bytes 524288 | tf_op jit(solution)/shard_map/all_to_all | solution.py:476
  28.3 17.9 %copy-start = (bf16[4,3,2,4,4096]{4,3,2,1,0:T(4,128)(2,1)S(1)}, bf16[4,3,2,4,4096]{4,3,2,1,0:T(4,128)(2,1)}, u32[]{:S(2)}) copy-start(bf16[4,3,2,4,4096]{4,3,2,1,0:T(4,128)(2,1)} %history.1) | copy-start | bytes 2359300
  28.3 17.9 %copy-start.7 = (bf16[1664,256]{1,0:T(8,128)(2,1)S(1)}, bf16[1664,256]{1,0:T(8,128)(2,1)}, u32[]{:S(2)}) copy-start(bf16[1664,256]{1,0:T(8,128)(2,1)} %constant.5.clone.mats) | copy-start | bytes 2555908
  28.3 17.2 %collective-permute-start.3 = (s32[4,4096]{1,0:T(4,128)S(1)}, s32[4,4096]{1,0:T(4,128)S(1)}, u32[]{:S(2)}, u32[]{:S(2)}) collective-permute-start(s32[4,4096]{1,0:T(4,128)S(1)} %copy-done.5), channel_id=1, source_target_pairs={{0,255},{1,254},{2,253},{3,252},{4,251},{5,250},{6,249},{7,248},{8... | collective-permute-start | bytes 196616 | tf_op jit(solution)/shard_map/ppermute | solution.py:483
  37.4 8.8 %collective-permute-start.4 = (s32[4,4096]{1,0:T(4,128)S(1)}, s32[4,4096]{1,0:T(4,128)S(1)}, u32[]{:S(2)}, u32[]{:S(2)}) collective-permute-start(s32[4,4096]{1,0:T(4,128)S(1)} %copy-done.5), channel_id=1, source_target_pairs={{255,1},{254,2},{253,3},{252,4},{251,5},{250,6},{249,7},{248,8},{2... | collective-permute-start | bytes 196616 | tf_op jit(solution)/shard_map/ppermute | solution.py:485
  38.8 10.4 %collective-permute-start = (f32[64,256]{1,0:T(8,128)S(1)}, f32[64,256]{1,0:T(8,128)S(1)}, u32[]{:S(2)}, u32[]{:S(2)}) collective-permute-start(f32[64,256]{1,0:T(8,128)S(1)} %get-tuple-element.24), channel_id=1, source_target_pairs={{0,1},{1,2},{2,3},{3,0},{4,5},{5,6},{6,7},{7,4},{8,9},{9,10},{10,1... | collective-permute-start | bytes 196616 | tf_op jit(solution)/shard_map/ppermute | solution.py:499
  38.9 10.3 %collective-permute-start.1 = (f32[64,256]{1,0:T(8,128)S(1)}, f32[64,256]{1,0:T(8,128)S(1)}, u32[]{:S(2)}, u32[]{:S(2)}) collective-permute-start(f32[64,256]{1,0:T(8,128)S(1)} %get-tuple-element.25), channel_id=1, source_target_pairs={{0,2},{1,3},{2,0},{3,1},{4,6},{5,7},{6,4},{7,5},{8,10},{9,11},{10,... | collective-permute-start | bytes 196616 | tf_op jit(solution)/shard_map/ppermute | solution.py:499
  40.3 9.0 %collective-permute-start.2 = (f32[64,256]{1,0:T(8,128)S(1)}, f32[64,256]{1,0:T(8,128)S(1)}, u32[]{:S(2)}, u32[]{:S(2)}) collective-permute-start(f32[64,256]{1,0:T(8,128)S(1)} %get-tuple-element.26), channel_id=1, source_target_pairs={{0,3},{1,0},{2,1},{3,2},{4,7},{5,4},{6,5},{7,6},{8,11},{9,8},{10,9... | collective-permute-start | bytes 196616 | tf_op jit(solution)/shard_map/ppermute | solution.py:499

commit v6 on v4

--- a/solution.py
+++ b/solution.py
@@ -113,6 +113,51 @@
         ref[pl.ds(c, DEV, stride=len(blocks)), :] = jnp.concatenate([real, imag], 0).T
 
 
+def position():
+    return lax.axis_index("strike") * 4 + lax.axis_index("dip")
+
+
+def send_half(ref, field, angles, mats):
+    halves = ([], [])
+    lasts = []
+    lane = lax.broadcasted_iota(jnp.int32, (16, DEV), 1)
+    sign = 1.0 - 2.0 * (lane & 1).astype(F32)
+    for real, imag in dip_forward(field, angles):
+        lasts.append(jnp.sum(real[:16] * sign, 1, keepdims=True))
+        for rows, at in zip(halves, (0, 16)):
+            re, im = real[at : at + 32], imag[at : at + 32]
+            rows.append(jnp.concatenate([re, im], 1))
+            rows.append(jnp.concatenate([im, -re], 1))
+    outs = []
+    for rows, lanes in zip(halves, (slice(0, 128), slice(128, 256))):
+        table = (mats[: 2 * DEV, lanes], mats[2 * DEV : 4 * DEV, lanes])
+        outs.append(dot3(split(jnp.concatenate(rows, 0)), table))
+    out = jnp.concatenate(outs, 1)
+    pieces = []
+    for c, last in enumerate(lasts):
+        pieces.append(out[64 * c : 64 * c + 32])
+        pieces.append(jnp.where(lane == 0, last, out[64 * c + 32 : 64 * c + 48]))
+        pieces.append(out[64 * c + 48 : 64 * c + 64])
+    ref[...] = jnp.concatenate(pieces, 0).T
+
+
+def receive_half(ref):
+    device = position()
+    low = jnp.where(device < DEV // 2, 1.0, 0.0)
+    zero = jnp.where(device == 0, 1.0, 0.0)
+    up = 1.0 - low
+    lines = ref[...].T
+    blocks = []
+    for c in range(2):
+        line = lines[64 * c : 64 * c + 64]
+        ar, br, ai, bi = [line[16 * i : 16 * i + 16] for i in range(4)]
+        none = jnp.zeros_like(ar)
+        real = [low * ar, low * br + up * ar, up * br + zero * ai, none]
+        imag = [(low - zero) * ai, low * bi + up * ai, up * bi, none]
+        blocks.append((jnp.concatenate(real, 0), jnp.concatenate(imag, 0)))
+    return blocks
+
+
 def turns(angles):
     cos = [angles[32 + m : 33 + m, :] for m in range(4)]
     sin = [angles[36 + m : 37 + m, :] for m in range(4)]
@@ -136,16 +181,21 @@
     return blocks
 
 
-def dip_inverse(blocks, angles):
+def dip_inverse(lines, angles, mats, packed):
     cos, sin = turns(angles)
+    lane = lax.broadcasted_iota(jnp.int32, (16, DEV), 1)
+    sign = (1.0 - 2.0 * (lane & 1).astype(F32)) * (1.0 / math.sqrt(NZ))
+    lasts = [imag[:16, :1] for _, imag in lines]
     field = []
-    for real, imag in blocks:
+    for (real, imag), last in zip(long_dft(lines, mats, 1), lasts):
         re = [real[16 * m : 16 * m + 16] for m in range(4)]
         im = [imag[16 * m : 16 * m + 16] for m in range(4)]
         u = [cos[m] * re[m] - sin[m] * im[m] for m in range(4)]
         v1 = cos[1] * im[1] + sin[1] * re[1]
         v3 = cos[3] * im[3] + sin[3] * re[3]
         a, b, c, d = u[0] + u[2], u[0] - u[2], u[1] + u[3], v3 - v1
+        if packed:
+            a, b = a + sign * last, b + sign * last
         field.append(jnp.concatenate([a + c, b + d, a - c, b - d], 0))
     return field
 
@@ -190,16 +240,16 @@
         for c in range(3):
             fields[c, rows, :] = part[16 * c : 16 * c + 16, :]
         state_out[rows, :] = part[48:64, :]
-    force = dip_inverse(long_dft(read_lines(lines, (0, 1, 2), 3), mats, 1), angles)
+    force = dip_inverse(read_lines(lines, (0, 1, 2), 3), angles, mats, False)
     opening[...] = 2.0 * force[2]
     rates, state = friction(force, (fields[0], fields[1]), fields[2], state_out[...])
     state_out[...] = state
     field = [[r[16 * d : 16 * d + 16] for d in range(4)] for r in rates]
-    write_lines(out, long_dft(dip_forward(field, angles), mats, -1))
+    send_half(out, field, angles, mats)
 
 
 def last_kernel(lines, fields, state_in, opening, angles, mats, out):
-    force = dip_inverse(long_dft(read_lines(lines, (0, 1), 2), mats, 1), angles)
+    force = dip_inverse(read_lines(lines, (0, 1), 2), angles, mats, True)
     rates, state = friction(force, (fields[0], fields[1]), fields[2], state_in[...])
     for d in range(4):
         for c, value in enumerate(rates + [opening, state]):
@@ -214,11 +264,8 @@
         state[rows, :] = gathered[d, 48:64, :]
 
 
-def mixing(device):
-    shape = (64, DEV)
-    row = lax.broadcasted_iota(jnp.int32, shape, 0)
-    kx = (row >> 2) * DEV + lax.broadcasted_iota(jnp.int32, shape, 1)
-    kz = device * MODES + (row & 3)
+def mixing(kz, kx, lags):
+    shape = kz.shape
     mz = jnp.where(2 * kz < NZ, kz, kz - NZ)
     mx = jnp.where(2 * kx < NX, kx, kx - NX)
     qz = mz.astype(F32) * (2.0 * math.pi / NZ)
@@ -235,7 +282,7 @@
     before = [jnp.ones(shape, F32)] * 3
     now = first
     out = []
-    for lag in range(4):
+    for _ in range(lags):
         envelope = envelope * decay
         two, three, one = [envelope * c for c in now]
         out.append((xx * two + zz * three, xz * (two - three), zz * two + xx * three, one))
@@ -244,7 +291,7 @@
 
 
 def history_kernel(history, lengths, past1, past2, coef, held, reach):
-    device = lax.axis_index("strike") * 4 + lax.axis_index("dip")
+    device = position()
     for k1 in range(16):
         lanes = slice(DEV * k1, DEV * k1 + DEV)
         rows = slice(4 * k1, 4 * k1 + 4)
@@ -255,7 +302,22 @@
                 line = history[lag, c, part].astype(F32)
                 for k1 in range(16):
                     held[lag, c, part, 4 * k1 : 4 * k1 + 4, :] = line[:, DEV * k1 : DEV * k1 + DEV]
-    mix = mixing(device)
+    shape = (64, DEV)
+    row = lax.broadcasted_iota(jnp.int32, shape, 0)
+    kx = (row >> 2) * DEV + lax.broadcasted_iota(jnp.int32, shape, 1)
+    m = row & 3
+    mix = mixing(device * MODES + m, kx, 4)
+    origin = jnp.where(device == 0, 0, 64)
+    guest = (m + origin) == 2
+    upper = jnp.where(device < DEV // 2, 0, 1)
+    weight = jnp.where((m == upper) | (m == upper + 1), 2.0, 0.0)
+    weight = jnp.where(guest | ((m + origin) == 0), 1.0, weight)
+    cross = jnp.where((kx == NX // 2) & (weight == 2.0), 0.0, weight)
+    new = mixing(jnp.where(guest, NZ // 2, device * MODES + m), kx, 1)[0]
+    coef[7] = weight * new[0]
+    coef[8] = cross * new[1]
+    coef[9] = weight * new[2]
+    coef[10] = jnp.where(guest, 1.0, 0.0)
     length = reach[...]
     masked = [None] + [
         [jnp.where(length > float(lag), m, 0.0) for m in mix[lag]] for lag in range(1, 4)
@@ -294,7 +356,7 @@
     return dot3(inner, split(jnp.concatenate(turned, 1)))
 
 
-def lines_of(out, force, angles, mats):
+def back_to_rows(force, angles, mats):
     back = (mats[1152:1280, :128], mats[1152:1280, 128:])
     blocks = dot3(back, split(jnp.concatenate(force, 1)))
     cos = jnp.concatenate([angles[0:16, :]] * 4, 0)
@@ -303,7 +365,7 @@
     for c in range(len(force)):
         re, im = blocks[:64, DEV * c : DEV * c + DEV], blocks[64:, DEV * c : DEV * c + DEV]
         turned.append((re * cos - im * sin, im * cos + re * sin))
-    write_lines(out, long_dft(turned, mats, 1))
+    return long_dft(turned, mats, 1)
 
 
 def both_parts(coef, i):
@@ -321,13 +383,24 @@
     for c, f in enumerate(apply_mix(coef, 4, spec)):
         older[c] = f + past_next[c]
     force = apply_mix(coef, 0, spec) + [both_parts(coef, 3) * spec[:, 2 * DEV :]]
-    lines_of(out, [f + past[c] for c, f in enumerate(force)], angles, mats)
+    force = [f + past[c] for c, f in enumerate(force)]
+    write_lines(out, back_to_rows(force, angles, mats))
 
 
 def mode_kernel_second(lines, older, coef, angles, mats, out):
-    spec = spectrum_of(read_lines(lines, (0, 1), 2), angles, mats)
-    force = apply_mix(coef, 0, spec)
-    lines_of(out, [f + older[c] for c, f in enumerate(force)], angles, mats)
+    spec = spectrum_of(receive_half(lines), angles, mats)
+    guest = both_parts(coef, 10)
+    force = apply_mix(coef, 7, spec)
+    guests = [guest * f for f in force]
+    force = [f - g + older[c] for c, (f, g) in enumerate(zip(force, guests))]
+    extra = guests[0] + pltpu.roll(guests[1], 1, 0)
+    strike, dip, (alone, _) = back_to_rows(force + [extra], angles, mats)
+    zero = jnp.where(position() == 0, 1.0, 0.0)
+    blocks = []
+    for (real, imag), at in ((strike, 32), (dip, 48)):
+        head = (1.0 - zero) * imag[:16] + zero * alone[at : at + 16]
+        blocks.append((real, jnp.concatenate([head, imag[16:]], 0)))
+    write_lines(out, blocks)
 
 
 def call(kernel, outs, *args, scratch=(), grant=20, work=2.0):
@@ -350,7 +423,7 @@
 
 def shards(slip_rate, history, lengths, prestress, normal_stress, direct_effect, state_log):
     mats, angles = matrix_tables(), angle_tables()
-    three, two = (3 * DEV, 128), (2 * DEV, 128)
+    three, two, one = (3 * DEV, 128), (2 * DEV, 128), (DEV, 128)
     packed = slip_rate.reshape(3, 4, 16, 256).transpose(1, 0, 2, 3).reshape(4, 48, 256)
     slip = lax.all_to_all(packed, "dip", 0, 0, tiled=True)
     (out,) = call(first_kernel, [three], slip, angles, mats)
@@ -369,7 +442,7 @@
     ]
     past1, past2, coef = call(
         history_kernel,
-        [(3, 128, 256), (2, 128, 256), (7, 64, 256)],
+        [(3, 128, 256), (2, 128, 256), (11, 64, 256)],
         history,
         lengths,
         scratch=[pltpu.VMEM((3, 3, 2, 64, 256), F32), pltpu.VMEM((64, 256), F32)],
@@ -382,7 +455,7 @@
     )
     out, state, fields, opening = call(
         middle_kernel,
-        [two, (64, 256), (3, 64, 256), (64, 256)],
+        [one, (64, 256), (3, 64, 256), (64, 256)],
         exchange(out),
         *parts,
         angles,

time: 127 us -> 125 us (0.984)
  blocking collectives: 84.6 us -> 81.9 us
    all_to_all x3, blocking collectives: 66.5 us -> 63.9 us  [exchange(): lax.all_to_all(lines.reshape(DEV, 1, lanes), BOTH, 0, 0, tiled=True)]
  transfers between devices with their start and end apart: 4 -> 4, of which waited for: 2 -> 2; matrix products, arithmetic and copies ran while one was open for 0% -> 0% of each run, Pallas kernels for 1% -> 2%
where the time goes in v6:
time: 125 us
  blocking collectives  81.9 us (66%)
  starting transfers between devices  19.4 us (16%)
  waiting for transfers between devices  11.3 us (9%)
  Pallas kernels  10.2 us (8%)
    all_to_all x3, blocking collectives, exchange(): lax.all_to_all(lines.reshape(DEV, 1, lanes), BOTH, 0, 0, tiled=True)  63.9 us
    all_to_all x1, starting transfers between devices, exchange(): lax.all_to_all(lines.reshape(DEV, 1, lanes), BOTH, 0, 0, tiled=True)  14.4 us
    pallas_call x8, Pallas kernels, call(): pl.pallas_call(kernel, out_shape=[jax.ShapeDtypeStruct(s, F32) for s in o...  10.2 us
    all_to_all x1, waiting for transfers between devices, exchange(): lax.all_to_all(lines.reshape(DEV, 1, lanes), BOTH, 0, 0, tiled=True)  9.98 us
    all_to_all x1, blocking collectives, shards(): slip = lax.all_to_all(packed, 'dip', 0, 0, tiled=True)  9.81 us
    all_to_all x1, blocking collectives, shards(): gathered = lax.all_to_all(out, 'dip', 0, 0, tiled=True)  8.23 us
    ppermute x3, starting transfers between devices, shards(): lax.ppermute(part, 'dip', [(j, (j + i) % 4) for j in range(4)])  5.01 us
  transfers between devices with their start and end apart: 4, of which 2 were waited for; matrix products, arithmetic and copies ran while one was open for 0% of the time, Pallas kernels for 2%

profile of v6, /device:TPU:1, one launch (start us, length us, event | category | flops | bytes accessed | tf_op | source)
XLA Modules:
  0.0 124.6 jit_solution(17298563414077829689)
XLA Ops:
  0.6 0.0 copy-start.6
  0.6 1.0 copy.12
  1.6 0.0 copy-start.7
  1.7 9.8 %all_to_all.30.fields = f32[4,48,256]{2,1,0:T(8,128)S(1)} all-to-all(f32[4,48,256]{2,1,0:T(8,128)S(1)} %bitcast.21), channel_id=1, replica_groups=mesh['strike'=64,'dip'=4] {'dip'}, dimensions={0} | all-to-all | bytes 393216 | tf_op jit(solution)/shard_map/all_to_all | solution.py:428
  11.5 1.3 %shard_map.104 = f32[768,128]{1,0:T(8,128)} custom-call(f32[4,48,256]{2,1,0:T(8,128)S(1)} %all_to_all.30.fields, f32[40,256]{1,0:T(8,128)S(1)} %copy-done.7, bf16[1280,256]{1,0:T(8,128)(2,1)S(1)} %copy-done.6), custom_call_target="tpu_custom_call" | custom-call | flops 2000000000 | bytes 6000000 | tf_op jit(solution)/shard_map/pallas_call | solution.py:407
  12.8 14.4 %all-to-all-start.1 = ((f32[256,1,384]{2,1,0:T(1,128)}), f32[256,1,384]{2,1,0:T(1,128)S(1)}, u32[]{:S(2)}, u32[]{:S(2)}) async-start(f32[256,1,384]{2,1,0:T(1,128)} %bitcast.3), calls=%async_computation.1 | async-start | bytes 786432 | tf_op jit(solution)/shard_map/all_to_all | solution.py:420
  27.3 0.0 copy-start
  27.3 0.0 copy-start.5
  27.3 1.4 %collective-permute-start = (f32[64,256]{1,0:T(8,128)S(1)}, f32[64,256]{1,0:T(8,128)S(1)}, u32[]{:S(2)}, u32[]{:S(2)}) collective-permute-start(f32[64,256]{1,0:T(8,128)S(1)} %get-tuple-element.24), channel_id=1, source_target_pairs={{0,1},{1,2},{2,3},{3,0},{4,5},{5,6},{6,7},{7,4},{8,9},{9,10},{10,1... | collective-permute-start | bytes 196616 | tf_op jit(solution)/shard_map/ppermute | solution.py:440
  28.7 2.4 %collective-permute-start.1 = (f32[64,256]{1,0:T(8,128)S(1)}, f32[64,256]{1,0:T(8,128)S(1)}, u32[]{:S(2)}, u32[]{:S(2)}) collective-permute-start(f32[64,256]{1,0:T(8,128)S(1)} %get-tuple-element.25), channel_id=1, source_target_pairs={{0,2},{1,3},{2,0},{3,1},{4,6},{5,7},{6,4},{7,5},{8,10},{9,11},{10,... | collective-permute-start | bytes 196616 | tf_op jit(solution)/shard_map/ppermute | solution.py:440
  31.1 1.2 collective-permute-start.2
  32.3 2.1 %shard_map.106 = (f32[3,128,256]{2,1,0:T(8,128)S(1)}, f32[2,128,256]{2,1,0:T(8,128)S(1)}, f32[11,64,256]{2,1,0:T(8,128)S(1)}) custom-call(bf16[4,3,2,4,4096]{4,3,2,1,0:T(4,128)(2,1)S(1)} %copy-done, s32[4,4096]{1,0:T(4,128)S(1)} %copy-done.5), custom_call_target="tpu_custom_call" | custom-call | flops 2000000000 | bytes 6000000 | tf_op jit(solution)/shard_map/pallas_call | solution.py:407
  34.4 0.0 collective-permute-done.part1
  34.4 1.3 %collective-permute-done.1.part2 = f32[64,256]{1,0:T(8,128)S(1)} collective-permute-done((f32[64,256]{1,0:T(8,128)S(1)}, f32[64,256]{1,0:T(8,128)S(1)}, u32[]{:S(2)}, u32[]{:S(2)}) %collective-permute-start.1) | collective-permute-done | bytes 65568 | tf_op jit(solution)/shard_map/ppermute | solution.py:440
  35.7 10.0 %all-to-all-done.1 = f32[256,1,384]{2,1,0:T(1,128)S(1)} async-done(((f32[256,1,384]{2,1,0:T(1,128)}), f32[256,1,384]{2,1,0:T(1,128)S(1)}, u32[]{:S(2)}, u32[]{:S(2)}) %all-to-all-start.1) | async-done | bytes 393248 | tf_op jit(solution)/shard_map/all_to_all | solution.py:420
  45.7 2.1 %shard_map.107 = (f32[768,128]{1,0:T(8,128)S(1)}, f32[2,128,256]{2,1,0:T(8,128)S(1)}) custom-call(f32[768,128]{1,0:T(8,128)S(1)} %bitcast.14, f32[3,128,256]{2,1,0:T(8,128)S(1)} %get-tuple-element.31.past, f32[2,128,256]{2,1,0:T(8,128)S(1)} %get-tuple-element.32.past_next, f32[11,64,256]{2,1,0:T(8,128)S(1)} %get-tuple-element.33.coef, ...), custom_call_target="tpu_custom_call" | custom-call | flops 2000000000 | bytes 6000000 | tf_op jit(solution)/shard_map/pallas_call | solution.py:407
  47.7 24.0 %all_to_all.31 = f32[256,1,384]{2,1,0:T(1,128)S(1)} all-to-all(f32[256,1,384]{2,1,0:T(1,128)S(1)} %bitcast.16), channel_id=1, replica_groups=mesh['strike'=64,'dip'=4] {'strike','dip'}, dimensions={0} | all-to-all | bytes 786432 | tf_op jit(solution)/shard_map/all_to_all | solution.py:420
  71.7 1.5 %shard_map.108 = (f32[256,128]{1,0:T(8,128)S(1)}, f32[64,256]{1,0:T(8,128)S(1)}, f32[3,64,256]{2,1,0:T(8,128)S(1)}, f32[64,256]{1,0:T(8,128)S(1)}) custom-call(f32[768,128]{1,0:T(8,128)S(1)} %bitcast.15, f32[64,256]{1,0:T(8,128)S(1)} %get-tuple-element.35.part0, f32[64,256]{1,0:T(8,128)S(1)} %collective-permute-done.part1, ...), custom_call_target="tpu_custom_call" | custom-call | flops 2000000000 | bytes 6000000 | tf_op jit(solution)/shard_map/pallas_call | solution.py:407
  73.2 18.3 %all_to_all.32 = f32[256,1,128]{2,1,0:T(1,128)S(1)} all-to-all(f32[256,1,128]{2,1,0:T(1,128)S(1)} %bitcast.19), channel_id=1, replica_groups=mesh['strike'=64,'dip'=4] {'strike','dip'}, dimensions={0} | all-to-all | bytes 262144 | tf_op jit(solution)/shard_map/all_to_all | solution.py:420
  91.5 1.9 %shard_map.109 = f32[512,128]{1,0:T(8,128)S(1)} custom-call(f32[256,128]{1,0:T(8,128)S(1)} %bitcast.20, f32[2,128,256]{2,1,0:T(8,128)S(1)} %get-tuple-element.40.older, f32[11,64,256]{2,1,0:T(8,128)S(1)} %get-tuple-element.33.coef, f32[40,256]{1,0:T(8,128)S(1)} %copy-done.7, bf16[1280,256]{1,0:T(8,128)(2,1)S(1)} %copy-done.6), custom_call_target="tpu_custom_call" | custom-call | flops 2000000000 | bytes 6000000 | tf_op jit(solution)/shard_map/pallas_call | solution.py:407
  93.4 21.6 %all_to_all.33 = f32[256,1,256]{2,1,0:T(1,128)S(1)} all-to-all(f32[256,1,256]{2,1,0:T(1,128)S(1)} %bitcast.18), channel_id=1, replica_groups=mesh['strike'=64,'dip'=4] {'strike','dip'}, dimensions={0} | all-to-all | bytes 524288 | tf_op jit(solution)/shard_map/all_to_all | solution.py:420
  115.0 0.6 shard_map.110
  115.6 8.2 %all_to_all.34.gathered = f32[4,64,256]{2,1,0:T(8,128)S(1)} all-to-all(f32[4,64,256]{2,1,0:T(8,128)S(1)} %shard_map.110), channel_id=1, replica_groups=mesh['strike'=64,'dip'=4] {'dip'}, dimensions={0} | all-to-all | bytes 524288 | tf_op jit(solution)/shard_map/all_to_all | solution.py:468
  123.9 0.7 shard_map.111
  (14 shorter events, 0.1 us)
Async XLA Ops:
  0.6 10.8 %copy-start.6 = (bf16[1280,256]{1,0:T(8,128)(2,1)S(1)}, bf16[1280,256]{1,0:T(8,128)(2,1)}, u32[]{:S(2)}) copy-start(bf16[1280,256]{1,0:T(8,128)(2,1)} %constant.5.clone.mats) | copy-start | bytes 1966084
  1.6 9.8 %copy-start.7 = (f32[40,256]{1,0:T(8,128)S(1)}, f32[40,256]{1,0:T(8,128)}, u32[]{:S(2)}) copy-start(f32[40,256]{1,0:T(8,128)} %constant.4.clone.angles) | copy-start | bytes 122884
  12.8 14.4 %copy-start.1 = (f32[2,64,256]{2,1,0:T(8,128)S(1)}, f32[2,64,256]{2,1,0:T(8,128)}, u32[]{:S(2)}) copy-start(f32[2,64,256]{2,1,0:T(8,128)} %prestress.1) | copy-start | bytes 393220
  12.8 14.4 %copy-start.2 = (f32[64,256]{1,0:T(8,128)S(1)}, f32[64,256]{1,0:T(8,128)}, u32[]{:S(2)}) copy-start(f32[64,256]{1,0:T(8,128)} %normal.1) | copy-start | bytes 196612
  12.8 14.4 %copy-start.3 = (f32[64,256]{1,0:T(8,128)S(1)}, f32[64,256]{1,0:T(8,128)}, u32[]{:S(2)}) copy-start(f32[64,256]{1,0:T(8,128)} %effect.1) | copy-start | bytes 196612
  12.8 14.5 %copy-start.4 = (f32[64,256]{1,0:T(8,128)S(1)}, f32[64,256]{1,0:T(8,128)}, u32[]{:S(2)}) copy-start(f32[64,256]{1,0:T(8,128)} %state.1) | copy-start | bytes 196612
  12.8 32.9 %all-to-all-start.1 = ((f32[256,1,384]{2,1,0:T(1,128)}), f32[256,1,384]{2,1,0:T(1,128)S(1)}, u32[]{:S(2)}, u32[]{:S(2)}) async-start(f32[256,1,384]{2,1,0:T(1,128)} %bitcast.3), calls=%async_computation.1 | async-start | bytes 786432 | tf_op jit(solution)/shard_map/all_to_all | solution.py:420
  27.3 5.1 %copy-start = (bf16[4,3,2,4,4096]{4,3,2,1,0:T(4,128)(2,1)S(1)}, bf16[4,3,2,4,4096]{4,3,2,1,0:T(4,128)(2,1)}, u32[]{:S(2)}) copy-start(bf16[4,3,2,4,4096]{4,3,2,1,0:T(4,128)(2,1)} %history.1) | copy-start | bytes 2359300
  27.3 5.1 %copy-start.5 = (s32[4,4096]{1,0:T(4,128)S(1)}, s32[4,4096]{1,0:T(4,128)}, u32[]{:S(2)}) copy-start(s32[4,4096]{1,0:T(4,128)} %lengths.1) | copy-start | bytes 196612
  27.3 7.1 %collective-permute-start = (f32[64,256]{1,0:T(8,128)S(1)}, f32[64,256]{1,0:T(8,128)S(1)}, u32[]{:S(2)}, u32[]{:S(2)}) collective-permute-start(f32[64,256]{1,0:T(8,128)S(1)} %get-tuple-element.24), channel_id=1, source_target_pairs={{0,1},{1,2},{2,3},{3,0},{4,5},{5,6},{6,7},{7,4},{8,9},{9,10},{10,1... | collective-permute-start | bytes 196616 | tf_op jit(solution)/shard_map/ppermute | solution.py:440
  28.7 6.9 %collective-permute-start.1 = (f32[64,256]{1,0:T(8,128)S(1)}, f32[64,256]{1,0:T(8,128)S(1)}, u32[]{:S(2)}, u32[]{:S(2)}) collective-permute-start(f32[64,256]{1,0:T(8,128)S(1)} %get-tuple-element.25), channel_id=1, source_target_pairs={{0,2},{1,3},{2,0},{3,1},{4,6},{5,7},{6,4},{7,5},{8,10},{9,11},{10,... | collective-permute-start | bytes 196616 | tf_op jit(solution)/shard_map/ppermute | solution.py:440
  31.1 4.5 %collective-permute-start.2 = (f32[64,256]{1,0:T(8,128)S(1)}, f32[64,256]{1,0:T(8,128)S(1)}, u32[]{:S(2)}, u32[]{:S(2)}) collective-permute-start(f32[64,256]{1,0:T(8,128)S(1)} %get-tuple-element.26), channel_id=1, source_target_pairs={{0,3},{1,0},{2,1},{3,2},{4,7},{5,4},{6,5},{7,6},{8,11},{9,8},{10,9... | collective-permute-start | bytes 196616 | tf_op jit(solution)/shard_map/ppermute | solution.py:440
